TPU v7x, 32 devices: a whole 2x2x4 slice. The times are simulated.
32 devices in a mesh: clus: 8 (over y, x, core), col: 4 (over z).
Axes of the slice: x: 2, y: 2, z: 4, core: 2. Of those that a mesh axis runs over, the one named last changes fastest.
Arguments:
- density: bfloat16 [4096, 4096], P('clus', 'col'), may hold values from -6 to 6
- dens_pattern: int32 [16, 16], P('clus', 'col'), may hold values 0 or 1
- margin_window: bfloat16 [4096, 2048], P('col', 'clus'), may hold values from -0.09375 to 0.09375
- ovl_pattern: int32 [16, 8], P('col', 'clus'), may hold values 0 or 1
- keep_mask: int32 [8, 8], P('clus', 'col'), may hold values 0 or 1
- basis_values: bfloat16 [16, 256, 4096], P('col'), may hold values from -0.375 to 0.375
- rest_density: float32 [256, 256, 256], P('clus', 'col'), may hold values from -0.6 to 0.6
- slab_owner: int32 [16], replicated, may hold values from 0 to 7
- cell_lengths: float32 [3], replicated, may hold values from 200 to 260
Outputs:
- potential: float32 [256, 256, 256], P('clus', 'col')
- hartree: bfloat16 [4096, 4096], P('clus', 'col')
- product: bfloat16 [2048, 2048], P('clus', 'col')
All inputs are finite; a program needn't handle non-finite values. No bound on the sum of `dens_pattern` or of `ovl_pattern` or of `keep_mask` on one device may be relied on, other than what follows from the above.
Results may differ from a plain program's by a relative error of at most 0.0049.
Values may be sent and summed in bfloat16 or wider, within the bound.
No kernel may reach another device: no remote copies, remote signals or barrier semaphores. Data moves between devices by JAX's collectives and lax.ppermute only.
A program may use at most 128 MiB of HBM per device.

v0:
```python
import math

import jax
import jax.numpy as jnp
from jax import lax
from jax.sharding import PartitionSpec as P

B = 256
G = 256
BR_DEV = 2
QZ = 128


four_pi = 4.0 * math.pi
highest = lax.Precision.HIGHEST


def from_root(x, axis, root):
    mine = lax.axis_index(axis) == root
    return lax.psum(jnp.where(mine, x, jnp.zeros_like(x)), axis)


def green_values(cell_lengths, freq_x, freq_y, freq_z):

    def squared_wave(frequency, axis_pos):
        signed = jnp.where(frequency < G // 2, frequency, frequency - G).astype(jnp.float32)
        scaled = signed * (2.0 * math.pi) / cell_lengths[axis_pos]
        return scaled * scaled

    squared = squared_wave(freq_x, 0) + squared_wave(freq_y, 1) + squared_wave(freq_z, 2)
    at_anchor = (freq_x == 0) & (freq_y == 0) & (freq_z == 0)
    return jnp.where(at_anchor, 0.0, four_pi / jnp.where(at_anchor, 1.0, squared))


def dft_tables(length):
    counter = jnp.arange(length, dtype=jnp.int32)
    turn_count = (counter[:, None] * counter[None, :] % length).astype(jnp.float32)
    angles = turn_count * (2.0 * math.pi / length)
    return (jnp.cos(angles), jnp.sin(angles))


def matmul_high(left_side, right_side):
    return jnp.dot(left_side, right_side, precision=highest, preferred_element_type=jnp.float32)


def along_last(real_part, imag_part, cosine, sine_table, exp_sign):
    in_shape = real_part.shape
    lines_re = real_part.reshape(-1, in_shape[-1])
    lines_im = imag_part.reshape(-1, in_shape[-1])
    out_real = matmul_high(lines_re, cosine) - exp_sign * matmul_high(lines_im, sine_table)
    out_imag = matmul_high(lines_im, cosine) + exp_sign * matmul_high(lines_re, sine_table)
    return (out_real.reshape(in_shape), out_imag.reshape(in_shape))


def along_middle(real_part, imag_part, cosine, sine_table, exp_sign):

    def contract(matrix, values):
        return jnp.einsum(
            "axb,xu->aub", values, matrix, precision=highest, preferred_element_type=jnp.float32
        )

    out_real = contract(cosine, real_part) - exp_sign * contract(sine_table, imag_part)
    out_imag = contract(cosine, imag_part) + exp_sign * contract(sine_table, real_part)
    return (out_real, out_imag)


def per_device(
    density,
    dens_pattern,
    margin_window,
    ovl_pattern,
    keep_mask,
    basis_values,
    rest_density,
    slab_owner,
    cell_lengths,
):
    clus_count = lax.axis_size("clus")
    col_count = lax.axis_size("col")
    clus_index = lax.axis_index("clus")
    col_index = lax.axis_index("col")
    col_blocks = dens_pattern.shape[1]
    patch_cells = basis_values.shape[2]
    slice_cells = patch_cells // col_count
    lines_dev = slice_cells // QZ
    all_blocks = clus_count * BR_DEV
    plane_count = G // clus_count
    line_count = G // col_count
    ratio_cols = clus_count // col_count
    masked = (
        density.reshape(BR_DEV, B, col_blocks, B)
        * dens_pattern.astype(jnp.bfloat16)[:, None, :, None]
    ).reshape(BR_DEV * B, col_blocks * B)
    window_rows = masked[:B]
    margin_masked = (
        margin_window.reshape(col_blocks, B, B) * ovl_pattern.astype(jnp.bfloat16)[:, :, None]
    ).reshape(col_blocks * B, B)
    partial_sums = jnp.dot(
        window_rows,
        lax.all_gather(margin_masked, "clus", axis=1, tiled=True),
        preferred_element_type=jnp.float32,
    )
    summed = lax.psum_scatter(partial_sums, "col", scatter_dimension=1, tiled=True)
    keep_float = keep_mask.astype(jnp.float32)
    product = (
        (summed.reshape(B, ratio_cols, B) * keep_float[0][None, :, None])
        .reshape(B, ratio_cols * B)
        .astype(jnp.bfloat16)
    )
    phi_stack = basis_values.reshape(col_blocks * B, patch_cells)
    lifted = jnp.dot(masked, phi_stack, preferred_element_type=jnp.float32)
    root_col = clus_index * BR_DEV // col_blocks
    row_offset = clus_index * BR_DEV % col_blocks
    own_rows = lax.dynamic_slice_in_dim(basis_values, row_offset, BR_DEV, 0)
    row_basis = from_root(own_rows, "col", root_col)
    partial_rho = jnp.sum(
        row_basis.astype(jnp.float32) * lifted.reshape(BR_DEV, B, patch_cells), axis=1
    )
    slice_rho = lax.psum_scatter(partial_rho, "col", scatter_dimension=1, tiled=True)
    patch_rho = lax.all_gather(slice_rho, "clus", axis=0, tiled=True)
    line_ids = jnp.arange(all_blocks * lines_dev, dtype=jnp.int32)
    block_of_line = line_ids // lines_dev
    line_in_block = line_ids % lines_dev
    target = (
        block_of_line % plane_count * line_count
        + block_of_line // plane_count * lines_dev
        + line_in_block
    )
    owned = jnp.repeat(slab_owner == clus_index, lines_dev)
    cell_rows = jnp.arange(plane_count * line_count, dtype=jnp.int32)
    placer = ((cell_rows[:, None] == target[None, :]) & owned[None, :]).astype(jnp.float32)
    z_start = (G - QZ) // 2
    padded = jnp.pad(
        patch_rho.reshape(all_blocks * lines_dev, QZ), ((0, 0), (z_start, G - QZ - z_start))
    )
    grid_lines = matmul_high(placer, padded) + rest_density.reshape(plane_count * line_count, G)
    cosine, sine_table = dft_tables(G)
    real_z = matmul_high(grid_lines, cosine).reshape(plane_count, line_count, G)
    imag_z = (-matmul_high(grid_lines, sine_table)).reshape(plane_count, line_count, G)
    device_count = clus_count * col_count
    depth = G // device_count
    moved = (
        lax.all_to_all(
            real_z.transpose(2, 0, 1).reshape(G, plane_count * line_count),
            ("clus", "col"),
            split_axis=0,
            concat_axis=1,
            tiled=True,
        ),
        lax.all_to_all(
            imag_z.transpose(2, 0, 1).reshape(G, plane_count * line_count),
            ("clus", "col"),
            split_axis=0,
            concat_axis=1,
            tiled=True,
        ),
    )
    moved = [
        part.reshape(depth, clus_count, col_count, plane_count, line_count)
        .transpose(0, 1, 3, 2, 4)
        .reshape(depth, G, G)
        for part in moved
    ]
    real_y, imag_y = along_last(moved[0], moved[1], cosine, sine_table, -1.0)
    real_x, imag_x = along_middle(real_y, imag_y, cosine, sine_table, -1.0)
    freq_z = (clus_index * col_count + col_index) * depth + jnp.arange(depth, dtype=jnp.int32)[
        :, None, None
    ]
    freq_x = jnp.arange(G, dtype=jnp.int32)[None, :, None]
    freq_y = jnp.arange(G, dtype=jnp.int32)[None, None, :]
    factor = green_values(cell_lengths, freq_x, freq_y, freq_z)
    real_x, imag_x = along_middle(real_x * factor, imag_x * factor, cosine, sine_table, 1.0)
    real_y, imag_y = along_last(real_x, imag_x, cosine, sine_table, 1.0)
    moved = (
        lax.all_to_all(
            real_y.reshape(depth, clus_count, plane_count, col_count, line_count)
            .transpose(0, 1, 3, 2, 4)
            .reshape(depth, device_count * plane_count * line_count),
            ("clus", "col"),
            split_axis=1,
            concat_axis=0,
            tiled=True,
        ),
        lax.all_to_all(
            imag_y.reshape(depth, clus_count, plane_count, col_count, line_count)
            .transpose(0, 1, 3, 2, 4)
            .reshape(depth, device_count * plane_count * line_count),
            ("clus", "col"),
            split_axis=1,
            concat_axis=0,
            tiled=True,
        ),
    )
    back_real, back_imag = [
        part.reshape(G, plane_count, line_count).transpose(1, 2, 0) for part in moved
    ]
    back_lines_re = back_real.reshape(plane_count * line_count, G)
    back_lines_im = back_imag.reshape(plane_count * line_count, G)
    potential_lines = (
        matmul_high(back_lines_re, cosine) - matmul_high(back_lines_im, sine_table)
    ) / float(G * G * G)
    potential = potential_lines.reshape(plane_count, line_count, G)
    picked = lax.dot_general(
        placer,
        potential_lines,
        (((0,), (0,)), ((), ())),
        precision=highest,
        preferred_element_type=jnp.float32,
    )
    picked = picked[:, z_start : z_start + QZ].reshape(all_blocks, slice_cells)
    rows_mine = lax.psum_scatter(picked, "clus", scatter_dimension=0, tiled=True)
    patch_pot = lax.all_gather(rows_mine, "col", axis=1, tiled=True)
    weighted = (
        (row_basis.astype(jnp.float32) * patch_pot[:, None, :])
        .astype(jnp.bfloat16)
        .reshape(BR_DEV * B, patch_cells)
    )
    hartree_full = lax.dot_general(
        weighted, phi_stack, (((1,), (1,)), ((), ())), preferred_element_type=jnp.float32
    )
    hartree = (
        (
            hartree_full.reshape(BR_DEV, B, col_blocks, B)
            * dens_pattern.astype(jnp.float32)[:, None, :, None]
        )
        .reshape(BR_DEV * B, col_blocks * B)
        .astype(jnp.bfloat16)
    )
    return (potential, hartree, product)


def solution(mesh):
    in_specs = (
        P("clus", "col"),
        P("clus", "col"),
        P("col", "clus"),
        P("col", "clus"),
        P("clus", "col"),
        P("col", None, None),
        P("clus", "col", None),
        P(),
        P(),
    )
    out_specs = (P("clus", "col", None), P("clus", "col"), P("clus", "col"))
    return jax.shard_map(
        per_device, mesh=mesh, in_specs=in_specs, out_specs=out_specs, check_vma=False
    )
```

profile of v0, /device:TPU:0, one launch (start us, length us, event | category | flops | bytes accessed | tf_op | source)
XLA Modules:
  0.0 678.3 jit_solution(16320235742992901187)
XLA Ops:
  8.1 4.5 dynamic-slice_select_fusion
  14.4 156.0 %all-reduce.5.cloned.1.call-done = bf16[2,256,4096]{2,1,0:T(8,128)(2,1)} async-done(((bf16[2,256,4096]{2,1,0:T(8,128)(2,1)}), bf16[2,256,4096]{2,1,0:T(8,128)(2,1)}) %all-reduce.5.cloned.1.call-update) | async-done | bytes 4194320 | tf_op jit(solution)/shard_map/psum | solution.py:20
  170.4 8.8 %fusion = f32[2,4096]{1,0:T(2,128)S(1)} fusion(bf16[2,256,4096]{2,1,0:T(8,128)(2,1)} %all-reduce.5.cloned.1.call-done, bf16[2,256,1024]{2,1,0:T(8,128)(2,1)S(1)} %bitcast.159, bf16[1024,4096,1]{1,0,2:T(8,128)(2,1)} %bitcast.157), kind=kOutput, calls=%fused_computation.2 | convolution fusion | flops 4301250560 | bytes 13664256 | tf_op jit(solution)/shard_map/dot_general | solution.py:111
  181.2 42.7 %reduce-scatter.7.cloned.1.call-done = f32[1024,2]{1,0:T(8,128)} async-done(((f32[4096,2]{1,0:T(8,128)}), f32[1024,2]{1,0:T(8,128)}) %reduce-scatter.7.cloned.1.call-update) | async-done | bytes 8208
  225.2 9.2 %all-gather = f32[8,2,1024]{2,1,0:T(2,128)S(1)} all-gather(f32[1,2,1024]{2,1,0:T(2,128)S(1)} %bitcast.163), channel_id=1, replica_groups=mesh['clus'=8,'col'=4] {'clus'}, dimensions={0}, use_global_device_ids=true | all-gather | bytes 73728 | tf_op jit(solution)/shard_map/all_gather | solution.py:120
  237.1 4.1 convolution_negate_fusion
  241.2 5.6 copy.25
  246.8 5.0 all_to_all.51
  251.8 3.7 all-to-all-start.1
  255.4 4.1 fusion.59
  259.5 5.6 copy.23
  265.1 5.0 all_to_all.48
  270.1 32.2 %all-to-all-done.1 = f32[32,8,2048]{2,1,0:T(8,128)} async-done(((f32[32,8,2048]{2,1,0:T(8,128)}), f32[32,8,2048]{2,1,0:T(8,128)}, u32[]{:S(2)}, u32[]{:S(2)}) %all-to-all-start.1) | async-done | bytes 2097184 | tf_op jit(solution)/shard_map/all_to_all | solution.py:150
  302.3 4.6 all-to-all-start
  311.0 4.9 reshape.303
  315.9 8.2 %copy.48 = f32[8,8,4,32,64]{4,2,3,1,0:T(4,128)} copy(f32[8,8,4,32,64]{4,3,0,2,1:T(8,128)} %reshape.303) | data formatting | bytes 4194304 | tf_op jit(solution)/shard_map/reshape | solution.py:159
  324.1 4.2 reshape_reshape.13
  328.3 4.1 fusion.54
  332.3 21.3 %all-to-all-done = f32[32,8,2048]{2,1,0:T(8,128)} async-done(((f32[32,8,2048]{2,1,0:T(8,128)}), f32[32,8,2048]{2,1,0:T(8,128)}, u32[]{:S(2)}, u32[]{:S(2)}) %all-to-all-start) | async-done | bytes 2097184 | tf_op jit(solution)/shard_map/all_to_all | solution.py:143
  353.6 5.3 reshape.301
  358.9 8.1 %copy.49 = f32[8,8,4,32,64]{4,2,3,1,0:T(4,128)} copy(f32[8,8,4,32,64]{4,3,0,2,1:T(8,128)} %reshape.301) | data formatting | bytes 4194304 | tf_op jit(solution)/shard_map/reshape | solution.py:159
  367.0 5.3 reshape_reshape.12
  372.3 4.6 fusion.57
  385.5 3.7 bitcast_multiply_fusion
  395.0 3.5 bitcast_multiply_fusion.1
  411.9 4.3 convolution_add_fusion
  416.2 5.1 reshape_reshape.15
  421.3 4.7 copy.46
  426.0 5.0 all_to_all.57
  430.9 4.1 copy.31
  435.1 5.1 all-to-all-start.3
  440.2 4.4 fusion.48
  444.6 4.1 convolution_subtract_fusion.1
  448.8 5.1 reshape_reshape.14
  453.9 4.7 copy.47
  458.5 3.6 all_to_all.54
  464.7 22.4 %all-to-all-done.3 = f32[8,32,2048]{2,0,1:T(8,128)} async-done(((f32[8,32,2048]{2,0,1:T(8,128)}), f32[8,32,2048]{2,0,1:T(8,128)}, u32[]{:S(2)}, u32[]{:S(2)}) %all-to-all-start.3) | async-done | bytes 2097184 | tf_op jit(solution)/shard_map/all_to_all | solution.py:184
  487.1 4.7 all-to-all-start.2
  493.1 4.8 fusion.162
  499.9 5.2 reshape.310
  505.0 3.6 copy.32
  508.6 62.0 %all-to-all-done.2 = f32[8,32,2048]{2,0,1:T(8,128)} async-done(((f32[8,32,2048]{2,0,1:T(8,128)}), f32[8,32,2048]{2,0,1:T(8,128)}, u32[]{:S(2)}, u32[]{:S(2)}) %all-to-all-start.2) | async-done | bytes 2097184 | tf_op jit(solution)/shard_map/all_to_all | solution.py:175
  570.6 4.9 reshape.308
  575.6 4.6 copy.29
  580.1 4.4 fusion.50
  592.6 52.8 %all-reduce.7.cloned.1.call-done = f32[16,1024]{1,0:T(8,128)} async-done(((f32[16,1024]{1,0:T(8,128)}), f32[16,1024]{1,0:T(8,128)}) %all-reduce.7.cloned.1.call-update) | async-done | bytes 65552
  646.1 13.4 %all_gather.10 = f32[2,4096]{1,0:T(2,128)S(1)} all-gather(f32[2,1024]{1,0:T(2,128)S(1)} %constant_dynamic-slice_fusion), channel_id=1, replica_groups=mesh['clus'=8,'col'=4] {'col'}, dimensions={1}, use_global_device_ids=true | all-gather | bytes 40960 | tf_op jit(solution)/shard_map/all_gather | solution.py:212
  659.5 9.2 %multiply_convert_fusion = bf16[2,256,4,256]{3,1,2,0:T(8,128)(2,1)S(1)} fusion(bf16[4,256,4096]{2,1,0:T(8,128)(2,1)} %param.14, bf16[2,256,4096]{2,1,0:T(8,128)(2,1)} %all-reduce.5.cloned.1.call-done, f32[2,4096]{1,0:T(2,128)S(1)} %all_gather.10, f32[2,4]{1,0:T(2,128)S(1)} %get-tuple-element.3), kind=kOutput, calls=%fused_computation.28 | convolution fusion | flops 4302307328 | bytes 13664288 | tf_op jit(solution)/shard_map/dot_general | solution.py:218
  (83 shorter events, 55.3 us)
Async XLA Ops:
  8.0 162.4 %all-reduce.5.cloned.1.call-start = ((), (), s32[]{:S(2)}) async-start(), calls=%async_computation.6 | async-start | bytes 8388608 | tf_op jit(solution)/shard_map/psum | solution.py:20
  12.5 0.7 copy-start.7
  12.6 1.2 copy-start.8
  12.6 1.4 copy-start.4
  12.6 211.4 %reduce-scatter.7.cloned.1.call-start = ((), (), s32[]{:S(2)}) async-start(), calls=%async_computation.9 | async-start | bytes 2621440
  251.8 50.6 %all-to-all-start.1 = ((f32[32,8,2048]{2,1,0:T(8,128)}), f32[32,8,2048]{2,1,0:T(8,128)}, u32[]{:S(2)}, u32[]{:S(2)}) async-start(f32[32,8,2048]{2,1,0:T(8,128)} %all_to_all.51), calls=%async_computation.1 | async-start | bytes 4194304 | tf_op jit(solution)/shard_map/all_to_all | solution.py:150
  270.1 36.9 %copy-start.9 = (s32[4,1]{0,1:T(1,128)S(1)}, s32[4,1]{0,1:T(1,128)}, u32[]{:S(2)}) copy-start(s32[4,1]{0,1:T(1,128)} %param.12) | copy-start | bytes 52
  270.1 37.0 %copy-start.5 = (bf16[1024,256]{1,0:T(8,128)(2,1)S(1)}, bf16[1024,256]{1,0:T(8,128)(2,1)}, u32[]{:S(2)}) copy-start(bf16[1024,256]{1,0:T(8,128)(2,1)} %param.11) | copy-start | bytes 1572868
  270.1 38.1 %copy-start.6 = (f32[3]{0:T(128)S(1)}, f32[3]{0:T(128)}, u32[]{:S(2)}) copy-start(f32[3]{0:T(128)} %param.17) | copy-start | bytes 40
  302.3 51.3 %all-to-all-start = ((f32[32,8,2048]{2,1,0:T(8,128)}), f32[32,8,2048]{2,1,0:T(8,128)}, u32[]{:S(2)}, u32[]{:S(2)}) async-start(f32[32,8,2048]{2,1,0:T(8,128)} %all_to_all.48), calls=%async_computation | async-start | bytes 4194304 | tf_op jit(solution)/shard_map/all_to_all | solution.py:143
  307.0 186.1 %all-gather.3.cloned.1.call-start = ((), (), s32[]{:S(2)}) async-start(), calls=%async_computation.7 | async-start | bytes 4718592 | tf_op jit(solution)/shard_map/all_gather | solution.py:100
  372.3 4.6 copy-start.1
  372.3 4.6 copy-start.2
  410.6 1.3 copy-start
  435.1 52.0 %all-to-all-start.3 = ((f32[8,32,2048]{2,0,1:T(8,128)}), f32[8,32,2048]{2,0,1:T(8,128)}, u32[]{:S(2)}, u32[]{:S(2)}) async-start(f32[8,32,2048]{2,0,1:T(8,128)} %copy.31), calls=%async_computation.3 | async-start | bytes 4194304 | tf_op jit(solution)/shard_map/all_to_all | solution.py:184
  487.1 83.6 %all-to-all-start.2 = ((f32[8,32,2048]{2,0,1:T(8,128)}), f32[8,32,2048]{2,0,1:T(8,128)}, u32[]{:S(2)}, u32[]{:S(2)}) async-start(f32[8,32,2048]{2,0,1:T(8,128)} %copy.28), calls=%async_computation.2 | async-start | bytes 4194304 | tf_op jit(solution)/shard_map/all_to_all | solution.py:175
  491.8 99.0 %reduce-scatter.5.cloned.1.call-start = ((), (), s32[]{:S(2)}) async-start(), calls=%async_computation.8 | async-start | bytes 2621440 | tf_op jit(solution)/shard_map/reduce_scatter | solution.py:103
  497.9 0.7 copy-start.10
  497.9 0.7 copy-start.11
  497.9 147.4 %all-reduce.7.cloned.1.call-start = ((), (), s32[]{:S(2)}) async-start(), calls=%async_computation.10 | async-start | bytes 131072
  587.4 1.3 copy-start.3
Sparse Core Ops, SparseCore 0:
  12.7 157.6 all-reduce.4
  181.3 42.5 reduce-scatter.6
  498.0 67.7 reduce-scatter.4
Sparse Core Ops, SparseCore 1:
  309.9 48.8 all-gather.2
  590.8 54.5 all-reduce.6
where the time goes:
time: 688 us; the launch traced here: 678 us
  waiting for transfers between devices  390 us (57%)
  local copies, waits for them, and re-layouts  123 us (18%)
  matrix products  97.4 us (14%)
  blocking collectives  22.6 us (3%)
  starting transfers between devices  18.3 us (3%)
  between operations  16.8 us (2%)
  other arithmetic  10.1 us (1%)
    psum x1, waiting for transfers between devices, from_root(): return lax.psum(jnp.where(mine, x, jnp.zeros_like(x)), axis)  156 us
    unnamed x7, waiting for transfers between devices  95.6 us
    all_to_all x1, waiting for transfers between devices, per_device(): lax.all_to_all(real_y.reshape(depth, clus_count, plane_count, col_count,...  62 us
    dot_general x13, matrix products, matmul_high(): jnp.dot(left_side, right_side, precision=highest, preferred_element_type=...  48.3 us
    all_to_all x1, waiting for transfers between devices, per_device(): lax.all_to_all(imag_z.transpose(2, 0, 1).reshape(G, plane_count * line_co...  32.2 us
    reshape x4, local copies, waits for them, and re-layouts, per_device(): part.reshape(depth, clus_count, col_count, plane_count, line_count)  26.5 us
    dot_general x8, matrix products, contract(): jnp.einsum('axb,xu->aub', values, matrix, precision=highest, preferred_el...  25.1 us
    all_to_all x1, waiting for transfers between devices, per_device(): lax.all_to_all(imag_y.reshape(depth, clus_count, plane_count, col_count,...  22.4 us
  transfers between devices with their start and end apart: 9, of which 7 were waited for; matrix products, arithmetic and copies ran while one was open for 25% of the time, Pallas kernels for 0%

commit v1 on v0

v1 whole, which is shorter than its diff:
```python
import math

import jax
import jax.numpy as jnp
import numpy as np
from jax import lax
from jax.experimental import pallas as pl
from jax.experimental.pallas import tpu as pltpu
from jax.sharding import PartitionSpec as P


QZ = 128
AXES = ("clus", "col")
HIGH = lax.Precision.HIGH


def cas_table(size):
    counter = np.arange(size)
    angles = (counter[:, None] * counter[None, :] % size) * (2.0 * math.pi / size)
    return (np.cos(angles) + np.sin(angles)).astype(np.float32)


def dot_high(equation, left_side, right_side):
    return jnp.einsum(
        equation, left_side, right_side, precision=HIGH, preferred_element_type=jnp.float32
    )


def exchange(values):
    return lax.all_to_all(values, AXES, split_axis=0, concat_axis=0, tiled=True)


def green_planes(cell_lengths, size, first, depth):
    def squared_wave(frequency, axis_pos):
        signed = jnp.where(frequency < size // 2, frequency, frequency - size).astype(jnp.float32)
        scaled = signed * (2.0 * math.pi) / cell_lengths[axis_pos]
        return scaled * scaled

    freq_z = first + jnp.arange(depth, dtype=jnp.int32)[:, None, None]
    freq_x = jnp.arange(size, dtype=jnp.int32)[None, :, None]
    freq_y = jnp.arange(size, dtype=jnp.int32)[None, None, :]
    squared = squared_wave(freq_x, 0) + squared_wave(freq_y, 1) + squared_wave(freq_z, 2)
    at_anchor = (freq_x == 0) & (freq_y == 0) & (freq_z == 0)
    return jnp.where(at_anchor, 0.0, 4.0 * math.pi / jnp.where(at_anchor, 1.0, squared))


def after(values, *others):
    return lax.optimization_barrier((values,) + others)[0]


def lift_kernel(order_ref, basis_ref, margin_ref, *refs, count):
    part_refs, lifted_ref, window_ref, held = refs[:count], refs[count], refs[count + 1], refs[count + 2]
    step = pl.program_id(0)
    for e in range(count):

        @pl.when(step == e)
        def _(e=e):
            held[...] = part_refs[e][...]

    block = margin_ref.shape[1]
    window_ref[0] = jnp.dot(
        held[:block, :], margin_ref[...], preferred_element_type=jnp.float32
    )

    @pl.loop(0, held.shape[0] // block)
    def _(i):
        at = pl.ds(pl.multiple_of(i * block, block), block)
        lifted_ref[0, at, :] = jnp.dot(
            held[at, :], basis_ref[...], preferred_element_type=jnp.float32
        )


def lift(order, basis, margin, parts):
    count = len(parts)
    height, depth = parts[0].shape
    width, block = basis.shape[1], margin.shape[1]
    once = pl.Buffered(1)
    whole = lambda i, s: (0, 0)
    return pl.pallas_call(
        lambda *refs: lift_kernel(*refs, count=count),
        out_shape=[
            jax.ShapeDtypeStruct((count, height, width), jnp.float32),
            jax.ShapeDtypeStruct((count, block, block), jnp.float32),
        ],
        grid_spec=pltpu.PrefetchScalarGridSpec(
            num_scalar_prefetch=1,
            grid=(count,),
            in_specs=[
                pl.BlockSpec((depth, width), whole, pipeline_mode=once),
                pl.BlockSpec((depth, block), whole, pipeline_mode=once),
            ]
            + [pl.BlockSpec((height, depth), whole, pipeline_mode=once) for _ in parts],
            out_specs=[
                pl.BlockSpec((1, height, width), lambda i, s: (s[i], 0, 0)),
                pl.BlockSpec((1, block, block), lambda i, s: (s[i], 0, 0)),
            ],
            scratch_shapes=[pltpu.VMEM((height, depth), jnp.bfloat16)],
        ),
        cost_estimate=pl.CostEstimate(
            flops=2 * height * depth * width * count,
            bytes_accessed=count * (2 * height * depth + 4 * height * width),
            transcendentals=0,
        ),
        name="lift",
    )(order, basis, margin, *parts)


def route_kernel(owner_ref, where_ref, part_ref, lifted_ref, *refs, pieces, outs):
    piece_refs, out_refs = refs[:pieces], refs[pieces : pieces + outs]
    rho_ref, held, in_sems, out_sems = refs[pieces + outs :]
    rows = held.shape[1]
    step = pl.program_id(0)

    @pl.when(step == 0)
    def _():
        for e in range(outs):
            start = part_ref[e] * rows
            for p in range(pieces):

                @pl.when(where_ref[e] == p)
                def _(e=e, p=p, start=start):
                    pltpu.make_async_copy(
                        piece_refs[p].at[pl.ds(start, rows)], held.at[e], in_sems.at[e]
                    ).start()

    pltpu.make_async_copy(
        piece_refs[0].at[pl.ds(0, rows)], held.at[step], in_sems.at[step]
    ).wait()
    for e in range(outs):

        @pl.when(step == e)
        def _(e=e):
            pltpu.make_async_copy(held.at[e], out_refs[e], out_sems.at[e]).start()

    for b in range(rows):
        basis = held[step, b].astype(jnp.float32)
        height = basis.shape[0]
        rho_ref[0, b : b + 1, :] = jnp.sum(
            basis * lifted_ref[0, b * height : (b + 1) * height, :], axis=0, keepdims=True
        )

    @pl.when(step == outs - 1)
    def _():
        for e in range(outs):
            pltpu.make_async_copy(held.at[e], out_refs[e], out_sems.at[e]).wait()


def route(owner, where, part, lifted, pieces, rows):
    outs = where.shape[0]
    shape = (rows,) + pieces[0].shape[1:]
    height, width = lifted.shape[1:]
    size = math.prod(shape) * outs
    return pl.pallas_call(
        lambda *refs: route_kernel(*refs, pieces=len(pieces), outs=outs),
        out_shape=[jax.ShapeDtypeStruct(shape, pieces[0].dtype)] * outs
        + [jax.ShapeDtypeStruct((outs, rows, width), jnp.float32)],
        grid_spec=pltpu.PrefetchScalarGridSpec(
            num_scalar_prefetch=3,
            grid=(outs,),
            in_specs=[pl.BlockSpec((1, height, width), lambda i, o, w, p: (o[i], 0, 0))]
            + [pl.BlockSpec(memory_space=pl.ANY)] * len(pieces),
            out_specs=[pl.BlockSpec(memory_space=pl.ANY)] * outs
            + [pl.BlockSpec((1, rows, width), lambda i, o, w, p: (o[i], 0, 0))],
            scratch_shapes=[
                pltpu.VMEM((outs,) + shape, pieces[0].dtype),
                pltpu.SemaphoreType.DMA((outs,)),
                pltpu.SemaphoreType.DMA((outs,)),
            ],
        ),
        cost_estimate=pl.CostEstimate(
            flops=2 * size, bytes_accessed=4 * size + 4 * size, transcendentals=0
        ),
        name="route",
    )(owner, where, part, lifted, *pieces)


def hartree_kernel(slot_ref, pattern_ref, pot_ref, columns_ref, *refs, count):
    row_refs, out_ref, scaled = refs[:count], refs[count], refs[count + 1]
    step = pl.program_id(0)
    rows, block, width = row_refs[0].shape

    @pl.when(step == 0)
    def _():
        for e in range(count):
            at = pl.ds(pl.multiple_of(slot_ref[e] * width, width), width)
            for b in range(rows):
                scaled[pl.ds(b * block, block), at] = (
                    row_refs[e][b].astype(jnp.float32) * pot_ref[b : b + 1, at]
                ).astype(jnp.bfloat16)

    @pl.loop(0, rows)
    def _(b):
        at = pl.ds(pl.multiple_of(b * block, block), block)
        keep = pattern_ref[b, step].astype(jnp.float32)
        values = lax.dot_general(
            scaled[at, :],
            columns_ref[...],
            (((1,), (1,)), ((), ())),
            preferred_element_type=jnp.float32,
        )
        out_ref[at, :] = (values * keep).astype(jnp.bfloat16)


def hartree_product(slots, pattern, pot, columns, row_parts):
    count = len(row_parts)
    rows, block, width = row_parts[0].shape
    depth, cells = columns.shape
    height = rows * block
    once = pl.Buffered(1)
    return pl.pallas_call(
        lambda *refs: hartree_kernel(*refs, count=count),
        out_shape=jax.ShapeDtypeStruct((height, depth), jnp.bfloat16),
        grid_spec=pltpu.PrefetchScalarGridSpec(
            num_scalar_prefetch=2,
            grid=(depth // block,),
            in_specs=[
                pl.BlockSpec(pot.shape, lambda i, s, p: (0, 0), pipeline_mode=once),
                pl.BlockSpec((block, cells), lambda i, s, p: (i, 0)),
            ]
            + [
                pl.BlockSpec((rows, block, width), lambda i, s, p: (0, 0, 0), pipeline_mode=once)
                for _ in row_parts
            ],
            out_specs=pl.BlockSpec((height, block), lambda i, s, p: (0, i)),
            scratch_shapes=[pltpu.VMEM((height, cells), jnp.bfloat16)],
        ),
        cost_estimate=pl.CostEstimate(
            flops=2 * height * depth * cells,
            bytes_accessed=2 * (depth + height) * cells,
            transcendentals=0,
        ),
        name="hartree",
    )(slots, pattern, pot, columns, *row_parts)


def make_program(clus_count, col_count):
    def pairs(move):
        return [
            (k * col_count + c, k2 * col_count + c2)
            for k in range(clus_count)
            for c in range(col_count)
            for k2, c2 in [move(k, c)]
            if 0 <= c2 < col_count
        ]

    def swap(values, distance):
        return lax.ppermute(values, AXES, pairs(lambda k, c: (k ^ distance, c)))

    even = [c ^ 1 for c in range(col_count)]
    odd = [c if c in (0, col_count - 1) else c - 1 if c % 2 == 0 else c + 1 for c in range(col_count)]
    moves = []
    holds = [list(range(col_count))]
    tips = [0, 0]
    while any(len({h[c] for h in holds}) < col_count for c in range(col_count)):
        made = []
        for kind, table in enumerate((even, odd)):
            arrived = [holds[tips[kind]][table[c]] for c in range(col_count)]
            if all(arrived[c] in [h[c] for h in holds] for c in range(col_count)):
                made.append(None)
                continue
            moves.append((kind, tips[kind]))
            holds.append(arrived)
            made.append(len(holds) - 1)
        tips = [made[1], made[0]]
    place = np.array(
        [[[h[c] for h in holds].index(o) for o in range(col_count)] for c in range(col_count)],
        np.int32,
    )

    def gather_line(values):
        arrays = [values]
        for kind, source in moves:
            table = (even, odd)[kind]
            arrays.append(lax.ppermute(arrays[source], AXES, pairs(lambda k, c: (k, table[c]))))
        return arrays

    def gather_clus(values):
        parts = {0: values}
        for e in list(range(2, clus_count, 2)) + list(range(1, clus_count, 2)):
            parts[e] = swap(parts[e ^ 1], 1) if e & 1 else swap(values, e)
        return [parts[e] for e in range(clus_count)]

    def per_device(
        density,
        dens_pattern,
        margin_window,
        ovl_pattern,
        keep_mask,
        basis_values,
        rest_density,
        slab_owner,
        cell_lengths,
    ):
        k = lax.axis_index("clus")
        c = lax.axis_index("col")
        rows, cols = dens_pattern.shape
        block = density.shape[0] // rows
        cells = basis_values.shape[2]
        all_blocks = clus_count * rows
        planes, lines, size = rest_density.shape
        devices = clus_count * col_count
        depth = size // devices
        slice_cells = cells // clus_count
        slice_lines = slice_cells // QZ
        patch_lines = cells // QZ
        lines_dev = patch_lines // col_count
        z_start = (size - QZ) // 2
        hartley = cas_table(size)
        hartley_q = jnp.asarray(hartley[z_start : z_start + QZ])
        line_id = np.arange(patch_lines)
        groups = max(1, all_blocks // planes)
        group_size = all_blocks // groups
        y_cells = (
            line_id[None, :] // lines_dev * lines
            + np.arange(groups)[:, None] * lines_dev
            + line_id[None, :] % lines_dev
        )
        hartley_y = jnp.asarray(hartley[y_cells])
        hartley = jnp.asarray(hartley)

        ratio = cols // rows
        device_id = k * col_count + c
        clus_ids = k ^ jnp.arange(clus_count, dtype=jnp.int32)

        own_phi = lax.dynamic_slice_in_dim(basis_values, k * slice_cells, slice_cells, 2)
        pieces = gather_line(own_phi)

        masked = (
            density.reshape(rows, block, cols, block)
            * dens_pattern.astype(jnp.bfloat16)[:, None, :, None]
        ).reshape(rows * block, cols * block)
        gathered = gather_clus(masked)

        rest_lines = rest_density.reshape(planes * lines, size)
        waves = dot_high("kz,lz->kl", hartley, rest_lines)
        moved = exchange((waves * 256.0).astype(jnp.float16).reshape(devices, depth, planes * lines))
        moved = after(moved, pieces[1], pieces[2])
        plane = (
            moved.reshape(clus_count, col_count, depth, planes, lines)
            .transpose(2, 0, 3, 1, 4)
            .reshape(depth, size, size)
            .astype(jnp.float32)
        )
        plane = dot_high("axy,yv->axv", plane, hartley)
        plane = dot_high("ux,axv->auv", hartley * (1.0 / 256.0), plane)

        phi_slice = own_phi.reshape(cols * block, slice_cells)
        margin_masked = (
            margin_window.reshape(cols, block, block)
            * ovl_pattern.astype(jnp.bfloat16)[:, :, None]
        ).reshape(cols * block, block)
        lifted, window = lift(clus_ids, phi_slice, margin_masked, gathered)
        where = jnp.asarray(place)[c][clus_ids // ratio]
        *sent, partial_rho = route(clus_ids, where, clus_ids % ratio, lifted, pieces, rows)
        patch_waves = dot_high(
            "qk,lq->kl", hartley_q, partial_rho.reshape(all_blocks * slice_lines, QZ)
        )
        patch_waves = patch_waves.reshape(devices, depth, all_blocks * slice_lines)
        patch_moved = exchange(patch_waves)
        patch_sum = jnp.sum(
            patch_moved.reshape(
                clus_count, col_count, depth, groups, group_size, slice_lines
            ),
            axis=1,
        )
        patch_sum = patch_sum.transpose(2, 3, 1, 0, 4).reshape(
            groups, group_size, depth, patch_lines
        )
        patch_y = dot_high("gizm,gmv->gizv", patch_sum, hartley_y)
        patch_y = patch_y.reshape(all_blocks, depth, size)
        block_ids = jnp.arange(all_blocks, dtype=jnp.int32)
        x_cells = slab_owner.astype(jnp.int32) * planes + block_ids % planes
        chosen = (x_cells[:, None] == jnp.arange(size, dtype=jnp.int32)[None, :]).astype(jnp.float32)
        hartley_x = jnp.einsum(
            "ix,xu->iu", chosen, hartley, precision=lax.Precision.HIGHEST
        )

        row_parts = []
        for e, part in enumerate(sent):
            row_parts.append(part if e == 0 else swap(part, e))

        plane = plane + dot_high("iu,izv->zuv", hartley_x, patch_y)

        factor = green_planes(cell_lengths, size, device_id * depth, depth) * (1.0 / size**3)
        plane = plane * factor

        picked = dot_high("iu,zuv->izv", hartley_x, plane).reshape(
            groups, group_size, depth, size
        )
        picked = dot_high("gizv,gmv->gizm", picked, hartley_y).reshape(
            clus_count, 1, rows, depth, patch_lines
        )
        picked = jnp.broadcast_to(picked, (clus_count, col_count, rows, depth, patch_lines))
        picked = exchange(picked.reshape(devices, rows, depth, patch_lines))
        patch_pot = dot_high("srdm,sdq->rmq", picked, hartley_q.T.reshape(devices, depth, QZ))
        patch_pot = patch_pot.reshape(rows, cells)

        plane = dot_high("xu,auv->axv", hartley, plane)
        plane = dot_high("axv,vy->axy", plane, hartley)
        back = (
            plane.astype(jnp.bfloat16)
            .reshape(depth, clus_count, planes, col_count, lines)
            .transpose(1, 3, 0, 2, 4)
            .reshape(devices, depth, planes * lines)
        )
        back = exchange(back).reshape(size, planes * lines)
        potential = dot_high("kl,kz->lz", back.astype(jnp.float32), hartley).reshape(
            planes, lines, size
        )

        hartree = hartree_product(
            clus_ids,
            dens_pattern,
            patch_pot,
            basis_values.reshape(cols * block, cells),
            row_parts,
        )

        span = clus_count // col_count
        window = (window * 32.0).astype(jnp.float16)
        window = lax.all_to_all(window, "clus", split_axis=0, concat_axis=0, tiled=True)
        window = window.reshape(col_count, span, block, block)
        summed = 0.0
        for step in range(col_count):
            part = lax.dynamic_index_in_dim(window, c ^ step, 0, keepdims=False)
            if step:
                part = lax.ppermute(part, AXES, pairs(lambda k, c: (k, c ^ step)))
            summed = summed + part.astype(jnp.float32)
        summed = summed * (keep_mask.astype(jnp.float32)[0][:, None, None] * (1.0 / 32.0))
        product = summed.transpose(1, 0, 2).reshape(block, span * block).astype(jnp.bfloat16)
        return (potential, hartree, product)

    return per_device


def solution(mesh):
    in_specs = (
        P("clus", "col"),
        P("clus", "col"),
        P("col", "clus"),
        P("col", "clus"),
        P("clus", "col"),
        P("col", None, None),
        P("clus", "col", None),
        P(),
        P(),
    )
    out_specs = (P("clus", "col", None), P("clus", "col"), P("clus", "col"))
    clus_count, col_count = mesh.shape["clus"], mesh.shape["col"]
    return jax.shard_map(
        make_program(clus_count, col_count),
        mesh=mesh,
        in_specs=in_specs,
        out_specs=out_specs,
        check_vma=False,
    )
```

time: 688 us -> 299 us (0.43); the launches traced: 678 us -> 297 us
  waiting for transfers between devices: 390 us -> 140 us
  local copies, waits for them, and re-layouts: 123 us -> 31.7 us
  matrix products: 97.4 us -> 21 us
  Pallas kernels: 0 us -> 37.8 us
  starting transfers between devices: 18.3 us -> 55.3 us
  blocking collectives: 22.6 us -> 0 us
  between operations: 16.8 us -> 1.09 us
    psum x1 -> x0, waiting for transfers between devices: 156 us -> none  [from_root(): return lax.psum(jnp.where(mine, x, jnp.zeros_like(x)), axis)]
    ppermute x0 -> x22, waiting for transfers between devices: none -> 130 us  [the longest x14 63.2 us: swap(): return lax.ppermute(values, AXES, pairs(lambda k, c: (k ^ distance, c)))]
    all_to_all x4 -> x5, waiting for transfers between devices: 138 us -> 9.93 us  [the longest x4 6.29 us: exchange(): return lax.all_to_all(values, AXES, split_axis=0, concat_axis=0, tiled=True)]
    unnamed x7 -> x0, waiting for transfers between devices: 95.6 us -> none
    dot_general x25 -> x13, matrix products: 97.4 us -> 21 us  [the longest x12 20.8 us: dot_high(): jnp.einsum(equation, left_side, right_side, precision=HIGH, preferred_ele...]
    pallas_call x0 -> x3, Pallas kernels: none -> 37.8 us  [the longest x1 16.3 us: lift(): pl.pallas_call(lambda *refs: lift_kernel(*refs, count=count), out_shape=[...]
    reshape x11 -> x6, local copies, waits for them, and re-layouts: 49.2 us -> 15 us  [the longest x3 7 us: per_device(): back = plane.astype(jnp.bfloat16).reshape(depth, clus_count, planes, col_...]
    ppermute x0 -> x22, starting transfers between devices: none -> 32 us  [the longest x5 16.4 us: gather_line(): lax.ppermute(arrays[source], AXES, pairs(lambda k, c: (k, table[c])))]
  transfers between devices with their start and end apart: 9 -> 27, of which waited for: 7 -> 12; matrix products, arithmetic and copies ran while one was open for 25% -> 18% of each run, Pallas kernels for 0% -> 9%
where the time goes in v1:
time: 299 us; the launch traced here: 297 us
  waiting for transfers between devices  140 us (47%)
  starting transfers between devices  55.3 us (18%)
  Pallas kernels  37.8 us (13%)
  local copies, waits for them, and re-layouts  31.7 us (11%)
  matrix products  21 us (7%)
  other arithmetic  9.79 us (3%)
    ppermute x14, waiting for transfers between devices, swap(): return lax.ppermute(values, AXES, pairs(lambda k, c: (k ^ distance, c)))  63.2 us
    ppermute x3, waiting for transfers between devices, per_device(): part = lax.ppermute(part, AXES, pairs(lambda k, c: (k, c ^ step)))  37 us
    ppermute x5, waiting for transfers between devices, gather_line(): lax.ppermute(arrays[source], AXES, pairs(lambda k, c: (k, table[c])))  30.1 us
    dot_general x12, matrix products, dot_high(): jnp.einsum(equation, left_side, right_side, precision=HIGH, preferred_ele...  20.8 us
    all_to_all x4, starting transfers between devices, exchange(): return lax.all_to_all(values, AXES, split_axis=0, concat_axis=0, tiled=True)  19.5 us
    ppermute x5, starting transfers between devices, gather_line(): lax.ppermute(arrays[source], AXES, pairs(lambda k, c: (k, table[c])))  16.4 us
    pallas_call x1, Pallas kernels, lift(): pl.pallas_call(lambda *refs: lift_kernel(*refs, count=count), out_shape=[...  16.3 us
    pallas_call x1, Pallas kernels, hartree_product(): pl.pallas_call(lambda *refs: hartree_kernel(*refs, count=count), out_shap...  11.1 us
  transfers between devices with their start and end apart: 27, of which 12 were waited for; matrix products, arithmetic and copies ran while one was open for 18% of the time, Pallas kernels for 9%

profile of v1, /device:TPU:0, one launch (start us, length us, event | category | flops | bytes accessed | tf_op | source)
XLA Modules:
  0.0 296.8 jit_solution(4812556849396496706)
XLA Ops:
  2.1 1.4 mul.148.refs_3_
  3.5 3.0 collective-permute-start.3
  6.5 1.5 collective-permute-start.5
  8.0 1.3 constant_dynamic-slice_fusion.1.refs_4_
  9.3 2.1 collective-permute-start
  11.4 1.6 collective-permute-start.1
  13.1 2.1 fusion.1
  15.2 5.9 %all-to-all-start = ((f16[32,8,2048]{2,1,0:T(8,128)(2,1)}), f16[32,8,2048]{2,1,0:T(8,128)(2,1)}, u32[]{:S(2)}, u32[]{:S(2)}) async-start(f16[32,8,2048]{2,1,0:T(8,128)(2,1)} %fusion.1), calls=%async_computation | async-start | bytes 2097152 | tf_op jit(solution)/shard_map/all_to_all | solution.py:30
  22.3 1.3 divide_multiply_fusion
  23.8 7.0 %collective-permute-done.3.refs_5_ = bf16[512,1024]{1,0:T(8,128)(2,1)} collective-permute-done((bf16[512,1024]{1,0:T(8,128)(2,1)}, bf16[512,1024]{1,0:T(8,128)(2,1)}, u32[]{:S(2)}, u32[]{:S(2)}) %collective-permute-start.3) | collective-permute-done | bytes 1048608 | tf_op jit(solution)/shard_map/ppermute | solution.py:247
  30.8 5.1 %collective-permute-done.refs_5_ = bf16[4,256,512]{2,1,0:T(8,128)(2,1)} collective-permute-done((bf16[4,256,512]{2,1,0:T(8,128)(2,1)S(1)}, bf16[4,256,512]{2,1,0:T(8,128)(2,1)}, u32[]{:S(2)}, u32[]{:S(2)}) %collective-permute-start) | collective-permute-done | bytes 1048608 | tf_op jit(solution)/shard_map/ppermute | solution.py:274
  35.9 9.4 %collective-permute-start.10 = (bf16[4,256,512]{2,1,0:T(8,128)(2,1)}, bf16[4,256,512]{2,1,0:T(8,128)(2,1)}, u32[]{:S(2)}, u32[]{:S(2)}) collective-permute-start(bf16[4,256,512]{2,1,0:T(8,128)(2,1)} %collective-permute-done.refs_5_), channel_id=1, source_target_pairs={{0,0},{1,2},{2,1},{3,3},{4,4},{5,6},{6,5},{7,7},{8,8},{9,10},{10,9... | collective-permute-start | bytes 3145736 | tf_op jit(solution)/shard_map/ppermute | solution.py:274
  46.9 14.4 %collective-permute-done.5.refs_7_ = bf16[512,1024]{1,0:T(8,128)(2,1)} collective-permute-done((bf16[512,1024]{1,0:T(8,128)(2,1)}, bf16[512,1024]{1,0:T(8,128)(2,1)}, u32[]{:S(2)}, u32[]{:S(2)}) %collective-permute-start.5) | collective-permute-done | bytes 1048608 | tf_op jit(solution)/shard_map/ppermute | solution.py:247
  61.4 4.0 %collective-permute-done.7.refs_9_ = bf16[512,1024]{1,0:T(8,128)(2,1)} collective-permute-done((bf16[512,1024]{1,0:T(8,128)(2,1)}, bf16[512,1024]{1,0:T(8,128)(2,1)}, u32[]{:S(2)}, u32[]{:S(2)}) %collective-permute-start.7) | collective-permute-done | bytes 1048608 | tf_op jit(solution)/shard_map/ppermute | solution.py:247
  69.0 3.4 %reshape.306 = f16[8,4,8,32,64]{4,3,2,1,0:T(8,128)(2,1)S(1)} reshape(f16[32,8,2048]{2,1,0:T(8,128)(2,1)} %all-to-all-done) | data formatting | bytes 2097152 | tf_op jit(solution)/shard_map/reshape | solution.py:339
  72.4 4.0 %copy.39 = f16[8,8,32,4,64]{4,3,2,1,0:T(4,128)(2,1)} copy(f16[8,8,32,4,64]{4,2,0,3,1:T(8,128)(2,1)S(1)} %bitcast.105) | data formatting | bytes 2097152 | tf_op jit(solution)/shard_map/transpose | solution.py:340
  76.4 3.8 %reshape.307 = f16[8,256,256]{2,1,0:T(8,128)(2,1)S(1)} reshape(f16[8,8,32,4,64]{4,3,2,1,0:T(4,128)(2,1)} %copy.39) | data formatting | bytes 2097152 | tf_op jit(solution)/shard_map/reshape | solution.py:341
  81.3 2.3 collective-permute-start.11
  84.6 2.3 fusion.30
  86.9 16.3 %lift.1 = (f32[8,512,512]{2,1,0:T(8,128)}, f32[8,256,256]{2,1,0:T(8,128)}) custom-call(s32[8]{0:T(128)} %get-tuple-element.34.refs_0_, bf16[1024,512]{1,0:T(8,128)(2,1)} %bitcast.107, bf16[1024,256]{1,0:T(8,128)(2,1)} %broadcast_multiply_fusion.refs_2_, bf16[512,1024]{1,0:T(8,128)(2,1)} %mul.148.refs_3_, bf16[512,1024]{1,0:T(8,128)(2,1)} %collective-permute-done.2.refs_4_, ...), custom_call_target="tpu_custom_call" | custom-call | flops 4294967296 | bytes 16777216 | tf_op jit(solution)/shard_map/lift/pallas_call | solution.py:79
  103.2 3.5 %collective-permute-done.9.refs_7_ = bf16[4,256,512]{2,1,0:T(8,128)(2,1)} collective-permute-done((bf16[4,256,512]{2,1,0:T(8,128)(2,1)}, bf16[4,256,512]{2,1,0:T(8,128)(2,1)}, u32[]{:S(2)}, u32[]{:S(2)}) %collective-permute-start.9) | collective-permute-done | bytes 1048608 | tf_op jit(solution)/shard_map/ppermute | solution.py:274
  106.7 21.5 %collective-permute-done.11.refs_9_ = bf16[4,256,512]{2,1,0:T(8,128)(2,1)} collective-permute-done((bf16[4,256,512]{2,1,0:T(8,128)(2,1)}, bf16[4,256,512]{2,1,0:T(8,128)(2,1)}, u32[]{:S(2)}, u32[]{:S(2)}) %collective-permute-start.11) | collective-permute-done | bytes 1048608 | tf_op jit(solution)/shard_map/ppermute | solution.py:274
  128.2 10.3 %route.1 = (bf16[2,256,512]{2,1,0:T(8,128)(2,1)}, bf16[2,256,512]{2,1,0:T(8,128)(2,1)}, bf16[2,256,512]{2,1,0:T(8,128)(2,1)}, bf16[2,256,512]{2,1,0:T(8,128)(2,1...) custom-call(s32[8]{0:T(128)} %get-tuple-element.34.refs_0_, ...), custom_call_target="tpu_custom_call" | custom-call | flops 4194304 | bytes 16777216 | tf_op jit(solution)/shard_map/route/pallas_call | solution.py:153
  140.4 5.0 %all-to-all-start.1 = ((f32[32,1,512]{2,1,0:T(1,128)}), f32[32,1,512]{2,1,0:T(1,128)S(1)}, u32[]{:S(2)}, u32[]{:S(2)}) async-start(f32[32,1,512]{2,1,0:T(1,128)} %reshape.339), calls=%async_computation.1 | async-start | bytes 131072 | tf_op jit(solution)/shard_map/all_to_all | solution.py:30
  146.6 6.3 %all-to-all-done.1 = f32[32,1,512]{2,1,0:T(1,128)S(1)} async-done(((f32[32,1,512]{2,1,0:T(1,128)}), f32[32,1,512]{2,1,0:T(1,128)S(1)}, u32[]{:S(2)}, u32[]{:S(2)}) %all-to-all-start.1) | async-done | bytes 65568 | tf_op jit(solution)/shard_map/all_to_all | solution.py:30
  152.9 3.8 %all-to-all-start.4 = ((f16[8,256,256]{2,1,0:T(8,128)(2,1)}), f16[8,256,256]{2,1,0:T(8,128)(2,1)S(1)}, u32[]{:S(2)}, u32[]{:S(2)}) async-start(f16[8,256,256]{2,1,0:T(8,128)(2,1)} %multiply_convert_fusion), calls=%async_computation.4 | async-start | bytes 2097152 | tf_op jit(solution)/shard_map/all_to_all | solution.py:421
  158.7 3.4 %fusion.4 = f32[8,256,256]{1,2,0:T(8,128)S(1)} fusion(f32[8,256,256]{2,1,0:T(8,128)} %fusion.30, f32[16,8,256]{2,0,1:T(8,128)S(1)} %fusion.16, f32[16,256,1]{1,0,2:T(8,128)S(1)} %convolution_bitcast_fusion.2, f32[8]{0:T(128)S(1)} %divide_multiply_fusion.2, f32[256,256]{0,1:T(8,128)} %broadcast_add_fusion, pred[256,256]{0,1:T(8,128)(4,1)S(1)} %broadcast_and_fusion, ...), kind=kOutput, calls=%fused_computation.8 | convolution fusion | flops 54525952 | bytes 4669480 | tf_op jit(solution)/shard_map/iu,izv->zuv/dot_general | solution.py:24
  164.1 1.7 reshape.341
  165.8 2.3 fusion.31
  168.1 3.6 %all-to-all-done.4 = f16[8,256,256]{2,1,0:T(8,128)(2,1)S(1)} async-done(((f16[8,256,256]{2,1,0:T(8,128)(2,1)}), f16[8,256,256]{2,1,0:T(8,128)(2,1)S(1)}, u32[]{:S(2)}, u32[]{:S(2)}) %all-to-all-start.4) | async-done | bytes 1048608 | tf_op jit(solution)/shard_map/all_to_all | solution.py:421
  172.8 2.6 all-to-all-start.3
  175.3 3.4 %fusion.7 = bf16[8,256,256]{2,1,0:T(8,128)(2,1)S(1)} fusion(f32[256,256,1]{1,0,2:T(8,128)S(1)} %copy-done.5, f32[8,256,256]{2,1,0:T(8,128)} %fusion.31), kind=kOutput, calls=%fused_computation.13 | convolution fusion | flops 805830656 | bytes 3407872 | tf_op jit(solution)/shard_map/axv,vy->axy/dot_general | solution.py:24
  179.6 1.8 copy.70
  181.4 4.3 %reshape.315 = bf16[32,8,2048]{2,1,0:T(8,128)(2,1)} reshape(bf16[8,4,8,32,64]{4,3,2,1,0:T(8,128)(2,1)} %bitcast.106) | data formatting | bytes 2097152 | tf_op jit(solution)/shard_map/reshape | solution.py:404
  185.8 6.1 %all-to-all-start.2 = ((bf16[32,8,2048]{2,1,0:T(8,128)(2,1)}), bf16[32,8,2048]{2,1,0:T(8,128)(2,1)S(1)}, u32[]{:S(2)}, u32[]{:S(2)}) async-start(bf16[32,8,2048]{2,1,0:T(8,128)(2,1)} %reshape.315), calls=%async_computation.2 | async-start | bytes 2097152 | tf_op jit(solution)/shard_map/all_to_all | solution.py:30
  191.9 1.6 collective-permute-start.13
  193.7 1.5 collective-permute-start.19
  195.3 2.4 collective-permute-start.20
  198.2 18.4 %collective-permute-done.19 = f16[2,256,256]{2,1,0:T(8,128)(2,1)S(1)} collective-permute-done((f16[2,256,256]{2,1,0:T(8,128)(2,1)S(1)}, f16[2,256,256]{2,1,0:T(8,128)(2,1)S(1)}, u32[]{:S(2)}, u32[]{:S(2)}) %collective-permute-start.19) | collective-permute-done | bytes 262176 | tf_op jit(solution)/shard_map/ppermute | solution.py:427
  216.6 18.7 %collective-permute-done.20 = f16[2,256,256]{2,1,0:T(8,128)(2,1)S(1)} collective-permute-done((f16[2,256,256]{2,1,0:T(8,128)(2,1)S(1)}, f16[2,256,256]{2,1,0:T(8,128)(2,1)S(1)}, u32[]{:S(2)}, u32[]{:S(2)}) %collective-permute-start.20) | collective-permute-done | bytes 262176 | tf_op jit(solution)/shard_map/ppermute | solution.py:427
  235.2 1.5 collective-permute-start.15
  236.7 1.5 collective-permute-start.17
  238.2 1.4 collective-permute-start.18
  243.4 29.4 %collective-permute-done.15.refs_8_ = bf16[2,256,512]{2,1,0:T(8,128)(2,1)} collective-permute-done((bf16[2,256,512]{2,1,0:T(8,128)(2,1)}, bf16[2,256,512]{2,1,0:T(8,128)(2,1)}, u32[]{:S(2)}, u32[]{:S(2)}) %collective-permute-start.15) | collective-permute-done | bytes 524320 | tf_op jit(solution)/shard_map/ppermute | solution.py:247
  272.8 8.2 %collective-permute-done.16.refs_9_ = bf16[2,256,512]{2,1,0:T(8,128)(2,1)} collective-permute-done((bf16[2,256,512]{2,1,0:T(8,128)(2,1)}, bf16[2,256,512]{2,1,0:T(8,128)(2,1)}, u32[]{:S(2)}, u32[]{:S(2)}) %collective-permute-start.16) | collective-permute-done | bytes 524320 | tf_op jit(solution)/shard_map/ppermute | solution.py:247
  281.1 11.1 %hartree.1 = bf16[512,1024]{1,0:T(8,128)(2,1)} custom-call(s32[8]{0:T(128)} %get-tuple-element.34.refs_0_, s32[2,4]{1,0:T(2,128)} %refs_1_.1, f32[2,4096]{1,0:T(2,128)} %bitcast.120, bf16[1024,4096]{1,0:T(8,128)(2,1)} %bitcast.119, bf16[2,256,512]{2,1,0:T(8,128)(2,1)} %get-tuple-element.18.refs_4_, bf16[2,256,512]{2,1,0:T(8,128)(2,1)} %collective-permute-done.12.refs_5_, ...), custom_call_target="tpu_custom_call" | custom-call | flops 4294967296 | bytes 12582912 | tf_op jit(solution)/shard_map/hartree/pallas_call | solution.py:210
  292.2 1.3 copy.47
  293.5 3.3 %fusion.32 = f32[32,64,256]{2,1,0:T(8,128)} fusion(bf16[32,64,256]{2,1,0:T(8,128)(2,1)} %bitcast.112, f32[256,256,1]{1,0,2:T(8,128)S(1)} %copy-done.5), kind=kOutput, calls=%fused_computation.72 | convolution fusion | flops 805306368 | bytes 3407872 | tf_op jit(solution)/shard_map/kl,kz->lz/dot_general | solution.py:24
  (106 shorter events, 23.3 us)
Async XLA Ops:
  0.6 12.4 %copy-start = (f32[32,64,256]{2,1,0:T(8,128)S(1)}, f32[32,64,256]{2,1,0:T(8,128)}, u32[]{:S(2)}) copy-start(f32[32,64,256]{2,1,0:T(8,128)} %param.19) | copy-start | bytes 6291460
  0.6 1.4 copy-start.7
  2.1 11.0 %copy-start.8 = (f32[256,256]{1,0:T(8,128)S(1)}, f32[256,256]{1,0:T(8,128)}, u32[]{:S(2)}) copy-start(f32[256,256]{1,0:T(8,128)} %constant.119.clone) | copy-start | bytes 786436
  3.5 27.3 %collective-permute-start.3 = (bf16[512,1024]{1,0:T(8,128)(2,1)}, bf16[512,1024]{1,0:T(8,128)(2,1)}, u32[]{:S(2)}, u32[]{:S(2)}) collective-permute-start(bf16[512,1024]{1,0:T(8,128)(2,1)} %mul.148.refs_3_), channel_id=1, source_target_pairs={{0,8},{1,9},{2,10},{3,11},{4,12},{5,13},{6,14},{7,15},{8,0},{9,1},... | collective-permute-start | bytes 3145736 | tf_op jit(solution)/shard_map/ppermute | solution.py:247
  6.5 54.9 %collective-permute-start.5 = (bf16[512,1024]{1,0:T(8,128)(2,1)}, bf16[512,1024]{1,0:T(8,128)(2,1)}, u32[]{:S(2)}, u32[]{:S(2)}) collective-permute-start(bf16[512,1024]{1,0:T(8,128)(2,1)} %mul.148.refs_3_), channel_id=1, source_target_pairs={{0,16},{1,17},{2,18},{3,19},{4,20},{5,21},{6,22},{7,23},{8,24},{9,... | collective-permute-start | bytes 3145736 | tf_op jit(solution)/shard_map/ppermute | solution.py:247
  8.0 57.4 %collective-permute-start.7 = (bf16[512,1024]{1,0:T(8,128)(2,1)}, bf16[512,1024]{1,0:T(8,128)(2,1)}, u32[]{:S(2)}, u32[]{:S(2)}) collective-permute-start(bf16[512,1024]{1,0:T(8,128)(2,1)} %mul.148.refs_3_), channel_id=1, source_target_pairs={{0,24},{1,25},{2,26},{3,27},{4,28},{5,29},{6,30},{7,31},{8,16},{9,... | collective-permute-start | bytes 3145736 | tf_op jit(solution)/shard_map/ppermute | solution.py:247
  9.3 5.9 %copy-start.2 = (bf16[4,256,512]{2,1,0:T(8,128)(2,1)}, bf16[4,256,512]{2,1,0:T(8,128)(2,1)S(1)}, u32[]{:S(2)}) copy-start(bf16[4,256,512]{2,1,0:T(8,128)(2,1)S(1)} %constant_dynamic-slice_fusion.1.refs_4_) | copy-start | bytes 3145732
  9.3 26.6 %collective-permute-start = (bf16[4,256,512]{2,1,0:T(8,128)(2,1)S(1)}, bf16[4,256,512]{2,1,0:T(8,128)(2,1)}, u32[]{:S(2)}, u32[]{:S(2)}) collective-permute-start(bf16[4,256,512]{2,1,0:T(8,128)(2,1)S(1)} %constant_dynamic-slice_fusion.1.refs_4_), channel_id=1, source_target_pairs={{0,1},{1,0},{2,3},{3,2},{4,5},{5,4},{6,7},{7,6},{8,9},{9,8},{10,11... | collective-permute-start | bytes 3145736 | tf_op jit(solution)/shard_map/ppermute | solution.py:274
  11.4 54.0 %collective-permute-start.1 = (bf16[4,256,512]{2,1,0:T(8,128)(2,1)S(1)}, bf16[4,256,512]{2,1,0:T(8,128)(2,1)}, u32[]{:S(2)}, u32[]{:S(2)}) collective-permute-start(bf16[4,256,512]{2,1,0:T(8,128)(2,1)S(1)} %constant_dynamic-slice_fusion.1.refs_4_), channel_id=1, source_target_pairs={{0,0},{1,2},{2,1},{3,3},{4,4},{5,6},{6,5},{7,7},{8,8},{9,10},{10,9... | collective-permute-start | bytes 3145736 | tf_op jit(solution)/shard_map/ppermute | solution.py:274
  13.0 8.6 %copy-start.14 = (f32[3]{0:T(128)S(1)}, f32[3]{0:T(128)}, u32[]{:S(2)}) copy-start(f32[3]{0:T(128)} %param.21) | copy-start | bytes 40
  13.0 10.6 %copy-start.15 = (s32[4,1]{0,1:T(1,128)S(1)}, s32[4,1]{0,1:T(1,128)}, u32[]{:S(2)}) copy-start(s32[4,1]{0,1:T(1,128)} %param.16) | copy-start | bytes 52
  13.0 10.6 %copy-start.16 = (s32[16]{0:T(128)S(1)}, s32[16]{0:T(128)}, u32[]{:S(2)}) copy-start(s32[16]{0:T(128)} %param.20) | copy-start | bytes 196
  15.2 52.8 %copy-start.9 = (bf16[1024,256]{1,0:T(8,128)(2,1)S(1)}, bf16[1024,256]{1,0:T(8,128)(2,1)}, u32[]{:S(2)}) copy-start(bf16[1024,256]{1,0:T(8,128)(2,1)} %param.15) | copy-start | bytes 1572868
  15.2 53.9 %all-to-all-start = ((f16[32,8,2048]{2,1,0:T(8,128)(2,1)}), f16[32,8,2048]{2,1,0:T(8,128)(2,1)}, u32[]{:S(2)}, u32[]{:S(2)}) async-start(f16[32,8,2048]{2,1,0:T(8,128)(2,1)} %fusion.1), calls=%async_computation | async-start | bytes 2097152 | tf_op jit(solution)/shard_map/all_to_all | solution.py:30
  30.8 49.5 %collective-permute-start.2 = (bf16[512,1024]{1,0:T(8,128)(2,1)}, bf16[512,1024]{1,0:T(8,128)(2,1)}, u32[]{:S(2)}, u32[]{:S(2)}) collective-permute-start(bf16[512,1024]{1,0:T(8,128)(2,1)} %mul.148.refs_3_), channel_id=1, source_target_pairs={{0,4},{1,5},{2,6},{3,7},{4,0},{5,1},{6,2},{7,3},{8,12},{9,13},{10,... | collective-permute-start | bytes 3145736 | tf_op jit(solution)/shard_map/ppermute | solution.py:247
  35.9 45.4 %collective-permute-start.10 = (bf16[4,256,512]{2,1,0:T(8,128)(2,1)}, bf16[4,256,512]{2,1,0:T(8,128)(2,1)}, u32[]{:S(2)}, u32[]{:S(2)}) collective-permute-start(bf16[4,256,512]{2,1,0:T(8,128)(2,1)} %collective-permute-done.refs_5_), channel_id=1, source_target_pairs={{0,0},{1,2},{2,1},{3,3},{4,4},{5,6},{6,5},{7,7},{8,8},{9,10},{10,9... | collective-permute-start | bytes 3145736 | tf_op jit(solution)/shard_map/ppermute | solution.py:274
  61.3 25.6 %collective-permute-start.4 = (bf16[512,1024]{1,0:T(8,128)(2,1)}, bf16[512,1024]{1,0:T(8,128)(2,1)}, u32[]{:S(2)}, u32[]{:S(2)}) collective-permute-start(bf16[512,1024]{1,0:T(8,128)(2,1)} %collective-permute-done.3.refs_5_), channel_id=1, source_target_pairs={{0,4},{1,5},{2,6},{3,7},{4,0},{5,1},{6,2},{7,3},{8,12},{9,13},{10,... | collective-permute-start | bytes 3145736 | tf_op jit(solution)/shard_map/ppermute | solution.py:247
  65.4 21.5 %collective-permute-start.6 = (bf16[512,1024]{1,0:T(8,128)(2,1)}, bf16[512,1024]{1,0:T(8,128)(2,1)}, u32[]{:S(2)}, u32[]{:S(2)}) collective-permute-start(bf16[512,1024]{1,0:T(8,128)(2,1)} %collective-permute-done.5.refs_7_), channel_id=1, source_target_pairs={{0,4},{1,5},{2,6},{3,7},{4,0},{5,1},{6,2},{7,3},{8,12},{9,13},{10,... | collective-permute-start | bytes 3145736 | tf_op jit(solution)/shard_map/ppermute | solution.py:247
  65.4 21.5 %collective-permute-start.8 = (bf16[512,1024]{1,0:T(8,128)(2,1)}, bf16[512,1024]{1,0:T(8,128)(2,1)}, u32[]{:S(2)}, u32[]{:S(2)}) collective-permute-start(bf16[512,1024]{1,0:T(8,128)(2,1)} %collective-permute-done.7.refs_9_), channel_id=1, source_target_pairs={{0,4},{1,5},{2,6},{3,7},{4,0},{5,1},{6,2},{7,3},{8,12},{9,13},{10,... | collective-permute-start | bytes 3145736 | tf_op jit(solution)/shard_map/ppermute | solution.py:247
  76.4 7.1 %copy-start.5 = (f32[256,256,1]{1,0,2:T(8,128)S(1)}, f32[256,256,1]{1,0,2:T(8,128)}, u32[]{:S(2)}) copy-start(f32[256,256,1]{1,0,2:T(8,128)} %constant.128) | copy-start | bytes 786436
  80.3 4.3 %copy-start.10 = (f32[256,256,1]{1,0,2:T(8,128)S(1)}, f32[256,256,1]{1,0,2:T(8,128)}, u32[]{:S(2)}) copy-start(f32[256,256,1]{1,0,2:T(8,128)} %constant.129) | copy-start | bytes 786436
  80.3 26.4 %collective-permute-start.9 = (bf16[4,256,512]{2,1,0:T(8,128)(2,1)}, bf16[4,256,512]{2,1,0:T(8,128)(2,1)}, u32[]{:S(2)}, u32[]{:S(2)}) collective-permute-start(bf16[4,256,512]{2,1,0:T(8,128)(2,1)} %collective-permute-done.1.refs_6_), channel_id=1, source_target_pairs={{0,1},{1,0},{2,3},{3,2},{4,5},{5,4},{6,7},{7,6},{8,9},{9,8},{10,11... | collective-permute-start | bytes 3145736 | tf_op jit(solution)/shard_map/ppermute | solution.py:274
  81.3 46.9 %collective-permute-start.11 = (bf16[4,256,512]{2,1,0:T(8,128)(2,1)}, bf16[4,256,512]{2,1,0:T(8,128)(2,1)}, u32[]{:S(2)}, u32[]{:S(2)}) collective-permute-start(bf16[4,256,512]{2,1,0:T(8,128)(2,1)} %collective-permute-done.10.refs_8_), channel_id=1, source_target_pairs={{0,1},{1,0},{2,3},{3,2},{4,5},{5,4},{6,7},{7,6},{8,9},{9,8},{10,11... | collective-permute-start | bytes 3145736 | tf_op jit(solution)/shard_map/ppermute | solution.py:274
  128.2 11.1 %copy-start.11 = (f32[128,256]{1,0:T(8,128)S(1)}, f32[128,256]{1,0:T(8,128)}, u32[]{:S(2)}) copy-start(f32[128,256]{1,0:T(8,128)} %constant.117.clone) | copy-start | bytes 393220
  128.2 17.2 %copy-start.6 = (f32[8,256,256]{2,1,0:T(8,128)S(1)}, f32[8,256,256]{2,1,0:T(8,128)}, u32[]{:S(2)}) copy-start(f32[8,256,256]{2,1,0:T(8,128)} %get-tuple-element.26) | copy-start | bytes 6291460
  140.4 12.5 %all-to-all-start.1 = ((f32[32,1,512]{2,1,0:T(1,128)}), f32[32,1,512]{2,1,0:T(1,128)S(1)}, u32[]{:S(2)}, u32[]{:S(2)}) async-start(f32[32,1,512]{2,1,0:T(1,128)} %reshape.339), calls=%async_computation.1 | async-start | bytes 131072 | tf_op jit(solution)/shard_map/all_to_all | solution.py:30
  146.6 11.8 %copy-start.13 = (f32[32,256,1]{1,0,2:T(8,128)S(1)}, f32[32,256,1]{1,0,2:T(8,128)}, u32[]{:S(2)}) copy-start(f32[32,256,1]{1,0,2:T(8,128)} %constant.130) | copy-start | bytes 98308
  152.9 18.9 %all-to-all-start.4 = ((f16[8,256,256]{2,1,0:T(8,128)(2,1)}), f16[8,256,256]{2,1,0:T(8,128)(2,1)S(1)}, u32[]{:S(2)}, u32[]{:S(2)}) async-start(f16[8,256,256]{2,1,0:T(8,128)(2,1)} %multiply_convert_fusion), calls=%async_computation.4 | async-start | bytes 2097152 | tf_op jit(solution)/shard_map/all_to_all | solution.py:421
  162.1 1.0 copy-start.12
  171.8 1.0 copy-start.3
  172.8 13.0 %all-to-all-start.3 = ((f32[32,1,512]{2,1,0:T(1,128)}), f32[32,1,512]{2,1,0:T(1,128)S(1)}, u32[]{:S(2)}, u32[]{:S(2)}) async-start(f32[32,1,512]{2,1,0:T(1,128)} %reshape.341), calls=%async_computation.3 | async-start | bytes 131072 | tf_op jit(solution)/shard_map/all_to_all | solution.py:30
  181.4 12.1 %copy-start.4 = (f16[8,256,256]{2,1,0:T(8,128)(2,1)S(1)}, f16[8,256,256]{2,1,0:T(8,128)(2,1)}, u32[]{:S(2)}) copy-start(f16[8,256,256]{2,1,0:T(8,128)(2,1)} %copy-done.3) | copy-start | bytes 3145732
  185.8 53.9 %copy-start.17 = (s32[1,2]{1,0:T(1,128)S(1)}, s32[1,2]{1,0:T(1,128)}, u32[]{:S(2)}) copy-start(s32[1,2]{1,0:T(1,128)} %param.17) | copy-start | bytes 28
  185.8 106.4 %all-to-all-start.2 = ((bf16[32,8,2048]{2,1,0:T(8,128)(2,1)}), bf16[32,8,2048]{2,1,0:T(8,128)(2,1)S(1)}, u32[]{:S(2)}, u32[]{:S(2)}) async-start(bf16[32,8,2048]{2,1,0:T(8,128)(2,1)} %reshape.315), calls=%async_computation.2 | async-start | bytes 2097152 | tf_op jit(solution)/shard_map/all_to_all | solution.py:30
  191.9 44.9 %collective-permute-start.12 = (bf16[2,256,512]{2,1,0:T(8,128)(2,1)}, bf16[2,256,512]{2,1,0:T(8,128)(2,1)}, u32[]{:S(2)}, u32[]{:S(2)}) collective-permute-start(bf16[2,256,512]{2,1,0:T(8,128)(2,1)} %get-tuple-element.19), channel_id=1, source_target_pairs={{0,4},{1,5},{2,6},{3,7},{4,0},{5,1},{6,2},{7,3},{8,12},{9,13},{10,... | collective-permute-start | bytes 1572872 | tf_op jit(solution)/shard_map/ppermute | solution.py:247
  191.9 46.3 %collective-permute-start.13 = (bf16[2,256,512]{2,1,0:T(8,128)(2,1)}, bf16[2,256,512]{2,1,0:T(8,128)(2,1)}, u32[]{:S(2)}, u32[]{:S(2)}) collective-permute-start(bf16[2,256,512]{2,1,0:T(8,128)(2,1)} %get-tuple-element.20), channel_id=1, source_target_pairs={{0,8},{1,9},{2,10},{3,11},{4,12},{5,13},{6,14},{7,15},{8,0},{9,1},... | collective-permute-start | bytes 1572872 | tf_op jit(solution)/shard_map/ppermute | solution.py:247
  193.7 22.8 %collective-permute-start.19 = (f16[2,256,256]{2,1,0:T(8,128)(2,1)S(1)}, f16[2,256,256]{2,1,0:T(8,128)(2,1)S(1)}, u32[]{:S(2)}, u32[]{:S(2)}) collective-permute-start(f16[2,256,256]{2,1,0:T(8,128)(2,1)S(1)} %get-tuple-element.27), channel_id=1, source_target_pairs={{0,1},{1,0},{2,3},{3,2},{4,5},{5,4},{6,7},{7,6},{8,9},{9,8},{10,11... | collective-permute-start | bytes 786440 | tf_op jit(solution)/shard_map/ppermute | solution.py:427
  195.3 40.0 %collective-permute-start.20 = (f16[2,256,256]{2,1,0:T(8,128)(2,1)S(1)}, f16[2,256,256]{2,1,0:T(8,128)(2,1)S(1)}, u32[]{:S(2)}, u32[]{:S(2)}) collective-permute-start(f16[2,256,256]{2,1,0:T(8,128)(2,1)S(1)} %get-tuple-element.29), channel_id=1, source_target_pairs={{0,2},{1,3},{2,0},{3,1},{4,6},{5,7},{6,4},{7,5},{8,10},{9,11},{10,... | collective-permute-start | bytes 786440 | tf_op jit(solution)/shard_map/ppermute | solution.py:427
  197.7 39.0 %collective-permute-start.21 = (f16[2,256,256]{2,1,0:T(8,128)(2,1)S(1)}, f16[2,256,256]{2,1,0:T(8,128)(2,1)S(1)}, u32[]{:S(2)}, u32[]{:S(2)}) collective-permute-start(f16[2,256,256]{2,1,0:T(8,128)(2,1)S(1)} %get-tuple-element.28), channel_id=1, source_target_pairs={{0,3},{1,2},{2,1},{3,0},{4,7},{5,6},{6,5},{7,4},{8,11},{9,10},{10,... | collective-permute-start | bytes 786440 | tf_op jit(solution)/shard_map/ppermute | solution.py:427
  216.6 26.8 %collective-permute-start.14 = (bf16[2,256,512]{2,1,0:T(8,128)(2,1)}, bf16[2,256,512]{2,1,0:T(8,128)(2,1)}, u32[]{:S(2)}, u32[]{:S(2)}) collective-permute-start(bf16[2,256,512]{2,1,0:T(8,128)(2,1)} %get-tuple-element.21), channel_id=1, source_target_pairs={{0,12},{1,13},{2,14},{3,15},{4,8},{5,9},{6,10},{7,11},{8,4},{9,5},... | collective-permute-start | bytes 1572872 | tf_op jit(solution)/shard_map/ppermute | solution.py:247
  235.2 37.6 %collective-permute-start.15 = (bf16[2,256,512]{2,1,0:T(8,128)(2,1)}, bf16[2,256,512]{2,1,0:T(8,128)(2,1)}, u32[]{:S(2)}, u32[]{:S(2)}) collective-permute-start(bf16[2,256,512]{2,1,0:T(8,128)(2,1)} %get-tuple-element.22), channel_id=1, source_target_pairs={{0,16},{1,17},{2,18},{3,19},{4,20},{5,21},{6,22},{7,23},{8,24},{9,... | collective-permute-start | bytes 1572872 | tf_op jit(solution)/shard_map/ppermute | solution.py:247
  236.7 44.3 %collective-permute-start.16 = (bf16[2,256,512]{2,1,0:T(8,128)(2,1)}, bf16[2,256,512]{2,1,0:T(8,128)(2,1)}, u32[]{:S(2)}, u32[]{:S(2)}) collective-permute-start(bf16[2,256,512]{2,1,0:T(8,128)(2,1)} %get-tuple-element.23), channel_id=1, source_target_pairs={{0,20},{1,21},{2,22},{3,23},{4,16},{5,17},{6,18},{7,19},{8,28},{9,... | collective-permute-start | bytes 1572872 | tf_op jit(solution)/shard_map/ppermute | solution.py:247
  236.7 44.3 %collective-permute-start.17 = (bf16[2,256,512]{2,1,0:T(8,128)(2,1)}, bf16[2,256,512]{2,1,0:T(8,128)(2,1)}, u32[]{:S(2)}, u32[]{:S(2)}) collective-permute-start(bf16[2,256,512]{2,1,0:T(8,128)(2,1)} %get-tuple-element.24), channel_id=1, source_target_pairs={{0,24},{1,25},{2,26},{3,27},{4,28},{5,29},{6,30},{7,31},{8,16},{9,... | collective-permute-start | bytes 1572872 | tf_op jit(solution)/shard_map/ppermute | solution.py:247
  238.2 42.8 %collective-permute-start.18 = (bf16[2,256,512]{2,1,0:T(8,128)(2,1)}, bf16[2,256,512]{2,1,0:T(8,128)(2,1)}, u32[]{:S(2)}, u32[]{:S(2)}) collective-permute-start(bf16[2,256,512]{2,1,0:T(8,128)(2,1)} %get-tuple-element.25), channel_id=1, source_target_pairs={{0,28},{1,29},{2,30},{3,31},{4,24},{5,25},{6,26},{7,27},{8,20},{9,... | collective-permute-start | bytes 1572872 | tf_op jit(solution)/shard_map/ppermute | solution.py:247
  292.2 4.6 %copy-start.1 = (f32[32,64,256]{2,1,0:T(8,128)S(1)}, f32[32,64,256]{2,1,0:T(8,128)}, u32[]{:S(2)}) copy-start(f32[32,64,256]{2,1,0:T(8,128)} %param.19) | copy-start | bytes 6291460

commit v2 on v1

--- a/solution.py
+++ b/solution.py
@@ -48,14 +48,15 @@
     return lax.optimization_barrier((values,) + others)[0]
 
 
-def lift_kernel(order_ref, basis_ref, margin_ref, *refs, count):
-    part_refs, lifted_ref, window_ref, held = refs[:count], refs[count], refs[count + 1], refs[count + 2]
+def lift_kernel(order_ref, basis_ref, margin_ref, *refs, places, held_before):
+    part_refs = refs[: len(places)]
+    lifted_ref, window_ref, held = refs[len(places) + held_before :]
     step = pl.program_id(0)
-    for e in range(count):
+    for part_ref, (e, start) in zip(part_refs, places):
 
         @pl.when(step == e)
-        def _(e=e):
-            held[...] = part_refs[e][...]
+        def _(part_ref=part_ref, start=start):
+            held[start : start + part_ref.shape[0], :] = part_ref[...]
 
     block = margin_ref.shape[1]
     window_ref[0] = jnp.dot(
@@ -70,17 +71,25 @@
         )
 
 
-def lift(order, basis, margin, parts):
-    count = len(parts)
-    height, depth = parts[0].shape
+def lift(order, basis, margin, parts, total, before=()):
+    count = order.shape[0]
+    pieces = [piece for part in parts for piece in part]
+    places = []
+    for e, part in enumerate(parts):
+        start = 0
+        for piece in part:
+            places.append((e, start))
+            start += piece.shape[0]
+    height, depth = start, pieces[0].shape[1]
     width, block = basis.shape[1], margin.shape[1]
     once = pl.Buffered(1)
     whole = lambda i, s: (0, 0)
+    first_before = 3 + len(pieces)
     return pl.pallas_call(
-        lambda *refs: lift_kernel(*refs, count=count),
+        lambda *refs: lift_kernel(*refs, places=places, held_before=len(before)),
         out_shape=[
-            jax.ShapeDtypeStruct((count, height, width), jnp.float32),
-            jax.ShapeDtypeStruct((count, block, block), jnp.float32),
+            jax.ShapeDtypeStruct((total, height, width), jnp.float32),
+            jax.ShapeDtypeStruct((total, block, block), jnp.float32),
         ],
         grid_spec=pltpu.PrefetchScalarGridSpec(
             num_scalar_prefetch=1,
@@ -89,20 +98,22 @@
                 pl.BlockSpec((depth, width), whole, pipeline_mode=once),
                 pl.BlockSpec((depth, block), whole, pipeline_mode=once),
             ]
-            + [pl.BlockSpec((height, depth), whole, pipeline_mode=once) for _ in parts],
+            + [pl.BlockSpec(piece.shape, whole, pipeline_mode=once) for piece in pieces]
+            + [pl.BlockSpec(memory_space=pl.ANY) for _ in before],
             out_specs=[
                 pl.BlockSpec((1, height, width), lambda i, s: (s[i], 0, 0)),
                 pl.BlockSpec((1, block, block), lambda i, s: (s[i], 0, 0)),
             ],
             scratch_shapes=[pltpu.VMEM((height, depth), jnp.bfloat16)],
         ),
+        input_output_aliases={first_before + i: i for i in range(len(before))},
         cost_estimate=pl.CostEstimate(
             flops=2 * height * depth * width * count,
             bytes_accessed=count * (2 * height * depth + 4 * height * width),
             transcendentals=0,
         ),
         name="lift",
-    )(order, basis, margin, *parts)
+    )(order, basis, margin, *pieces, *before)
 
 
 def route_kernel(owner_ref, where_ref, part_ref, lifted_ref, *refs, pieces, outs):
@@ -251,11 +262,15 @@
     moves = []
     holds = [list(range(col_count))]
     tips = [0, 0]
-    while any(len({h[c] for h in holds}) < col_count for c in range(col_count)):
+    while any(len({h[c] for h in holds} - {-1}) < col_count for c in range(col_count)):
         made = []
         for kind, table in enumerate((even, odd)):
-            arrived = [holds[tips[kind]][table[c]] for c in range(col_count)]
-            if all(arrived[c] in [h[c] for h in holds] for c in range(col_count)):
+            if tips[kind] is None:
+                made.append(None)
+                continue
+            source = holds[tips[kind]]
+            arrived = [-1 if table[c] == c else source[table[c]] for c in range(col_count)]
+            if all(arrived[c] in [-1] + [h[c] for h in holds] for c in range(col_count)):
                 made.append(None)
                 continue
             moves.append((kind, tips[kind]))
@@ -271,13 +286,23 @@
         arrays = [values]
         for kind, source in moves:
             table = (even, odd)[kind]
-            arrays.append(lax.ppermute(arrays[source], AXES, pairs(lambda k, c: (k, table[c]))))
+            moved = pairs(lambda k, c: (k, table[c]) if table[c] != c else (k ^ 1, c))
+            arrays.append(lax.ppermute(arrays[source], AXES, moved))
         return arrays
 
     def gather_clus(values):
-        parts = {0: values}
-        for e in list(range(2, clus_count, 2)) + list(range(1, clus_count, 2)):
-            parts[e] = swap(parts[e ^ 1], 1) if e & 1 else swap(values, e)
+        half = values.shape[0] // 2
+        parts = {0: [values]}
+        evens = sorted(range(2, clus_count, 2), key=lambda e: bin(e).count("1"))
+        for e in evens + list(range(1, clus_count, 2)):
+            bits = [1 << b for b in range(clus_count.bit_length()) if e >> b & 1]
+            if e & 1:
+                parts[e] = [swap(piece, 1) for piece in parts[e ^ 1]]
+            elif len(bits) == 2:
+                first, second = parts[bits[0]][0], parts[bits[1]][0]
+                parts[e] = [swap(first[:half], bits[1]), swap(second[half:], bits[0])]
+            else:
+                parts[e] = [swap(values, e)]
         return [parts[e] for e in range(clus_count)]
 
     def per_device(
@@ -349,7 +374,13 @@
             margin_window.reshape(cols, block, block)
             * ovl_pattern.astype(jnp.bfloat16)[:, :, None]
         ).reshape(cols * block, block)
-        lifted, window = lift(clus_ids, phi_slice, margin_masked, gathered)
+        split = clus_count // 2
+        before = lift(
+            clus_ids[:split], phi_slice, margin_masked, gathered[:split], clus_count
+        )
+        lifted, window = lift(
+            clus_ids[split:], phi_slice, margin_masked, gathered[split:], clus_count, before
+        )
         where = jnp.asarray(place)[c][clus_ids // ratio]
         *sent, partial_rho = route(clus_ids, where, clus_ids % ratio, lifted, pieces, rows)
         patch_waves = dot_high(
@@ -388,12 +419,14 @@
             groups, group_size, depth, size
         )
         picked = dot_high("gizv,gmv->gizm", picked, hartley_y).reshape(
-            clus_count, 1, rows, depth, patch_lines
-        )
-        picked = jnp.broadcast_to(picked, (clus_count, col_count, rows, depth, patch_lines))
-        picked = exchange(picked.reshape(devices, rows, depth, patch_lines))
-        patch_pot = dot_high("srdm,sdq->rmq", picked, hartley_q.T.reshape(devices, depth, QZ))
-        patch_pot = patch_pot.reshape(rows, cells)
+            clus_count, rows, depth, patch_lines
+        )
+        picked = picked.transpose(0, 2, 1, 3).reshape(clus_count, 1, depth, rows * patch_lines)
+        leading = lax.reduce_precision(picked, 8, 7)
+        picked = jnp.concatenate([leading, picked - leading], axis=-1).astype(jnp.bfloat16)
+        picked = jnp.broadcast_to(
+            picked, (clus_count, col_count, depth, 2 * rows * patch_lines)
+        ).reshape(devices, depth, 2 * rows * patch_lines)
 
         plane = dot_high("xu,auv->axv", hartley, plane)
         plane = dot_high("axv,vy->axy", plane, hartley)
@@ -403,10 +436,13 @@
             .transpose(1, 3, 0, 2, 4)
             .reshape(devices, depth, planes * lines)
         )
-        back = exchange(back).reshape(size, planes * lines)
-        potential = dot_high("kl,kz->lz", back.astype(jnp.float32), hartley).reshape(
-            planes, lines, size
-        )
+        back = jnp.concatenate([back, picked], axis=-1)
+        back = exchange(back).reshape(size, planes * lines + 2 * rows * patch_lines)
+        picked = back[:, planes * lines :].astype(jnp.float32).reshape(size, 2, rows, patch_lines)
+        patch_pot = dot_high("krm,qk->rmq", picked[:, 0] + picked[:, 1], hartley_q)
+        patch_pot = patch_pot.reshape(rows, cells)
+        back = back[:, : planes * lines].astype(jnp.float32)
+        potential = dot_high("kl,kz->lz", back, hartley).reshape(planes, lines, size)
 
         hartree = hartree_product(
             clus_ids,

time: 299 us -> 270 us (0.903)
  waiting for transfers between devices: 140 us -> 118 us
  starting transfers between devices: 55.3 us -> 48.1 us
  matrix products: 21 us -> 16.1 us
  Pallas kernels: 37.8 us -> 40.9 us
    ppermute x14 -> x16, waiting for transfers between devices: 63.2 us -> 35.5 us  [swap(): return lax.ppermute(values, AXES, pairs(lambda k, c: (k ^ distance, c)))]
    all_to_all x4 -> x3, waiting for transfers between devices: 6.29 us -> 18.9 us  [exchange(): return lax.all_to_all(values, AXES, split_axis=0, concat_axis=0, tiled=True)]
    all_to_all x4 -> x3, starting transfers between devices: 19.5 us -> 11.8 us  [exchange(): return lax.all_to_all(values, AXES, split_axis=0, concat_axis=0, tiled=True)]
    dot_general x12, matrix products: 20.8 us -> 15.9 us  [dot_high(): jnp.einsum(equation, left_side, right_side, precision=HIGH, preferred_ele...]
    slice x0 -> x3, local copies, waits for them, and re-layouts: none -> 4.45 us  [the longest x2 3.81 us: gather_clus(): parts[e] = [swap(first[:half], bits[1]), swap(second[half:], bits[0])]]
    all_to_all x1, waiting for transfers between devices: 3.65 us -> 0.01 us  [per_device(): lax.all_to_all(window, 'clus', split_axis=0, concat_axis=0, tiled=True)]
    ppermute x5, waiting for transfers between devices: 30.1 us -> 26.8 us  [gather_line(): arrays.append(lax.ppermute(arrays[source], AXES, moved))]
    pallas_call x1 -> x2, Pallas kernels: 16.3 us -> 19.3 us  [lift(): pl.pallas_call(lambda *refs: lift_kernel(*refs, places=places, held_befor...]
  transfers between devices with their start and end apart: 27 -> 28, of which waited for: 12 -> 8; matrix products, arithmetic and copies ran while one was open for 18% -> 20% of each run, Pallas kernels for 9% -> 7%
where the time goes in v2:
time: 270 us; the launch traced here: 269 us
  waiting for transfers between devices  118 us (44%)
  starting transfers between devices  48.1 us (18%)
  Pallas kernels  40.9 us (15%)
  local copies, waits for them, and re-layouts  33.5 us (12%)
  matrix products  16.1 us (6%)
  other arithmetic  11 us (4%)
    ppermute x3, waiting for transfers between devices, per_device(): part = lax.ppermute(part, AXES, pairs(lambda k, c: (k, c ^ step)))  36.9 us
    ppermute x16, waiting for transfers between devices, swap(): return lax.ppermute(values, AXES, pairs(lambda k, c: (k ^ distance, c)))  35.5 us
    ppermute x5, waiting for transfers between devices, gather_line(): arrays.append(lax.ppermute(arrays[source], AXES, moved))  26.8 us
    pallas_call x2, Pallas kernels, lift(): pl.pallas_call(lambda *refs: lift_kernel(*refs, places=places, held_befor...  19.3 us
    all_to_all x3, waiting for transfers between devices, exchange(): return lax.all_to_all(values, AXES, split_axis=0, concat_axis=0, tiled=True)  18.9 us
    dot_general x12, matrix products, dot_high(): jnp.einsum(equation, left_side, right_side, precision=HIGH, preferred_ele...  15.9 us
    ppermute x5, starting transfers between devices, gather_line(): arrays.append(lax.ppermute(arrays[source], AXES, moved))  14.9 us
    ppermute x16, starting transfers between devices, swap(): return lax.ppermute(values, AXES, pairs(lambda k, c: (k ^ distance, c)))  12.8 us
  transfers between devices with their start and end apart: 28, of which 8 were waited for; matrix products, arithmetic and copies ran while one was open for 20% of the time, Pallas kernels for 7%

profile of v2, /device:TPU:0, one launch (start us, length us, event | category | flops | bytes accessed | tf_op | source)
XLA Modules:
  0.0 268.8 jit_solution(611776011305775412)
XLA Ops:
  2.1 1.4 mul.148.refs_3_
  3.5 3.0 %collective-permute-start.4 = (bf16[512,1024]{1,0:T(8,128)(2,1)}, bf16[512,1024]{1,0:T(8,128)(2,1)}, u32[]{:S(2)}, u32[]{:S(2)}) collective-permute-start(bf16[512,1024]{1,0:T(8,128)(2,1)} %mul.148.refs_3_), channel_id=1, source_target_pairs={{0,8},{1,9},{2,10},{3,11},{4,12},{5,13},{6,14},{7,15},{8,0},{9,1},... | collective-permute-start | bytes 3145736 | tf_op jit(solution)/shard_map/ppermute | solution.py:258
  6.5 1.5 collective-permute-start.2
  8.0 1.3 constant_dynamic-slice_fusion.1.refs_4_
  9.3 1.6 collective-permute-start
  11.0 2.1 fusion.1
  13.1 3.8 %all-to-all-start = ((f16[32,8,2048]{2,1,0:T(8,128)(2,1)}), f16[32,8,2048]{2,1,0:T(8,128)(2,1)}, u32[]{:S(2)}, u32[]{:S(2)}) async-start(f16[32,8,2048]{2,1,0:T(8,128)(2,1)} %fusion.1), calls=%async_computation | async-start | bytes 2097152 | tf_op jit(solution)/shard_map/all_to_all | solution.py:30
  17.6 1.3 divide_multiply_fusion
  20.4 15.1 %collective-permute-done.refs_5_ = bf16[4,256,512]{2,1,0:T(8,128)(2,1)} collective-permute-done((bf16[4,256,512]{2,1,0:T(8,128)(2,1)S(1)}, bf16[4,256,512]{2,1,0:T(8,128)(2,1)}, u32[]{:S(2)}, u32[]{:S(2)}) %collective-permute-start) | collective-permute-done | bytes 1048608 | tf_op jit(solution)/shard_map/ppermute | solution.py:290
  37.0 1.9 slice.46
  40.1 1.2 gather_fusion
  42.4 1.9 slice.47
  45.0 12.9 %all-to-all-done = f16[32,8,2048]{2,1,0:T(8,128)(2,1)} async-done(((f16[32,8,2048]{2,1,0:T(8,128)(2,1)}), f16[32,8,2048]{2,1,0:T(8,128)(2,1)}, u32[]{:S(2)}, u32[]{:S(2)}) %all-to-all-start) | async-done | bytes 1048608 | tf_op jit(solution)/shard_map/all_to_all | solution.py:30
  57.9 3.4 %reshape.336 = f16[8,4,8,32,64]{4,3,2,1,0:T(8,128)(2,1)S(1)} reshape(f16[32,8,2048]{2,1,0:T(8,128)(2,1)} %all-to-all-done) | data formatting | bytes 2097152 | tf_op jit(solution)/shard_map/reshape | solution.py:364
  61.3 4.0 %copy.41 = f16[8,8,32,4,64]{4,3,2,1,0:T(4,128)(2,1)} copy(f16[8,8,32,4,64]{4,2,0,3,1:T(8,128)(2,1)S(1)} %bitcast.108) | data formatting | bytes 2097152 | tf_op jit(solution)/shard_map/transpose | solution.py:365
  65.3 3.8 %reshape.337 = f16[8,256,256]{2,1,0:T(8,128)(2,1)S(1)} reshape(f16[8,8,32,4,64]{4,3,2,1,0:T(4,128)(2,1)} %copy.41) | data formatting | bytes 2097152 | tf_op jit(solution)/shard_map/reshape | solution.py:366
  69.2 2.4 collective-permute-start.11
  71.5 10.9 %collective-permute-start.13 = (bf16[4,256,512]{2,1,0:T(8,128)(2,1)}, bf16[4,256,512]{2,1,0:T(8,128)(2,1)}, u32[]{:S(2)}, u32[]{:S(2)}) collective-permute-start(bf16[4,256,512]{2,1,0:T(8,128)(2,1)} %collective-permute-done.12.refs_8_), channel_id=1, source_target_pairs={{0,1},{1,0},{2,3},{3,2},{4,5},{5,4},{6,7},{7,6},{8,9},{9,8},{10,11... | collective-permute-start | bytes 3145736 | tf_op jit(solution)/shard_map/ppermute | solution.py:290
  84.0 2.3 fusion.36
  86.4 9.6 %lift.2 = (f32[8,512,512]{2,1,0:T(8,128)}, f32[8,256,256]{2,1,0:T(8,128)}) custom-call(s32[4]{0:T(128)} %get-tuple-element.39.refs_0_, bf16[1024,512]{1,0:T(8,128)(2,1)} %bitcast.106, bf16[1024,256]{1,0:T(8,128)(2,1)} %broadcast_multiply_fusion.refs_2_, bf16[512,1024]{1,0:T(8,128)(2,1)} %mul.148.refs_3_, bf16[512,1024]{1,0:T(8,128)(2,1)} %collective-permute-done.9.refs_4_, ...), custom_call_target="tpu_custom_call" | custom-call | flops 2147483648 | bytes 8388608 | tf_op jit(solution)/shard_map/lift/pallas_call | solution.py:88
  97.0 9.6 %lift.3 = (f32[8,512,512]{2,1,0:T(8,128)}, f32[8,256,256]{2,1,0:T(8,128)}) custom-call(s32[4]{0:T(128)} %get-tuple-element.40.refs_0_, bf16[1024,512]{1,0:T(8,128)(2,1)} %bitcast.107, bf16[1024,256]{1,0:T(8,128)(2,1)} %broadcast_multiply_fusion.refs_2_, ...), custom_call_target="tpu_custom_call", output_to_operand_aliasing={{0}: (9, {}), {1}: (10, {})} | custom-call | flops 2147483648 | bytes 8388608 | tf_op jit(solution)/shard_map/lift/pallas_call | solution.py:88
  106.6 11.7 %collective-permute-done.13.refs_9_ = bf16[4,256,512]{2,1,0:T(8,128)(2,1)} collective-permute-done((bf16[4,256,512]{2,1,0:T(8,128)(2,1)}, bf16[4,256,512]{2,1,0:T(8,128)(2,1)}, u32[]{:S(2)}, u32[]{:S(2)}) %collective-permute-start.13) | collective-permute-done | bytes 1048608 | tf_op jit(solution)/shard_map/ppermute | solution.py:290
  118.3 10.3 %route.1 = (bf16[2,256,512]{2,1,0:T(8,128)(2,1)}, bf16[2,256,512]{2,1,0:T(8,128)(2,1)}, bf16[2,256,512]{2,1,0:T(8,128)(2,1)}, bf16[2,256,512]{2,1,0:T(8,128)(2,1...) custom-call(s32[8]{0:T(128)} %copy-done.17, ...), custom_call_target="tpu_custom_call" | custom-call | flops 4194304 | bytes 16777216 | tf_op jit(solution)/shard_map/route/pallas_call | solution.py:164
  130.5 4.3 %all-to-all-start.1 = ((f32[32,1,512]{2,1,0:T(1,128)}), f32[32,1,512]{2,1,0:T(1,128)S(1)}, u32[]{:S(2)}, u32[]{:S(2)}) async-start(f32[32,1,512]{2,1,0:T(1,128)} %reshape.373), calls=%async_computation.1 | async-start | bytes 131072 | tf_op jit(solution)/shard_map/all_to_all | solution.py:30
  134.8 1.2 multiply_convert_fusion
  136.0 6.1 %all-to-all-done.1 = f32[32,1,512]{2,1,0:T(1,128)S(1)} async-done(((f32[32,1,512]{2,1,0:T(1,128)}), f32[32,1,512]{2,1,0:T(1,128)S(1)}, u32[]{:S(2)}, u32[]{:S(2)}) %all-to-all-start.1) | async-done | bytes 65568 | tf_op jit(solution)/shard_map/all_to_all | solution.py:30
  142.1 4.3 %all-to-all-start.3 = ((f16[8,256,256]{2,1,0:T(8,128)(2,1)}), f16[8,256,256]{2,1,0:T(8,128)(2,1)}, u32[]{:S(2)}, u32[]{:S(2)}) async-start(f16[8,256,256]{2,1,0:T(8,128)(2,1)} %multiply_convert_fusion), calls=%async_computation.3 | async-start | bytes 2097152 | tf_op jit(solution)/shard_map/all_to_all | solution.py:457
  148.3 3.4 %fusion.4 = f32[8,256,256]{1,2,0:T(8,128)S(1)} fusion(f32[8,256,256]{2,1,0:T(8,128)} %fusion.36, f32[16,8,256]{2,0,1:T(8,128)S(1)} %fusion.17, f32[16,256,1]{1,0,2:T(8,128)S(1)} %convolution_bitcast_fusion.3, f32[8]{0:T(128)S(1)} %divide_multiply_fusion.2, f32[256,256]{0,1:T(8,128)S(1)} %copy-done.12, pred[256,256]{0,1:T(8,128)(4,1)S(1)} %broadcast_and_fusion, ...), kind=kOutput, calls=%fused_computation.8 | convolution fusion | flops 54525952 | bytes 4669480 | tf_op jit(solution)/shard_map/iu,izv->zuv/dot_general | solution.py:24
  151.7 1.0 fusion.37
  153.7 1.9 fusion.7
  156.4 1.8 copy.69
  158.3 3.4 %reshape.345 = bf16[32,8,2048]{2,1,0:T(8,128)(2,1)S(1)} reshape(bf16[8,4,8,32,64]{4,3,2,1,0:T(8,128)(2,1)} %bitcast.109) | data formatting | bytes 2097152 | tf_op jit(solution)/shard_map/reshape | solution.py:437
  162.2 1.1 pad_maximum_fusion
  163.3 3.7 %all-to-all-start.2 = ((bf16[32,8,2176]{2,1,0:T(8,128)(2,1)}), bf16[32,8,2176]{2,1,0:T(8,128)(2,1)S(1)}, u32[]{:S(2)}, u32[]{:S(2)}) async-start(bf16[32,8,2176]{2,1,0:T(8,128)(2,1)} %pad_maximum_fusion), calls=%async_computation.2 | async-start | bytes 2228224 | tf_op jit(solution)/shard_map/all_to_all | solution.py:30
  167.1 1.6 collective-permute-start.15
  168.7 1.3 dynamic-slice_bitcast_fusion.2
  170.0 1.5 collective-permute-start.21
  171.5 2.4 collective-permute-start.22
  174.5 17.5 %collective-permute-done.21 = f16[2,256,256]{2,1,0:T(8,128)(2,1)S(1)} collective-permute-done((f16[2,256,256]{2,1,0:T(8,128)(2,1)S(1)}, f16[2,256,256]{2,1,0:T(8,128)(2,1)S(1)}, u32[]{:S(2)}, u32[]{:S(2)}) %collective-permute-start.21) | collective-permute-done | bytes 262176 | tf_op jit(solution)/shard_map/ppermute | solution.py:463
  192.4 19.3 %collective-permute-done.22 = f16[2,256,256]{2,1,0:T(8,128)(2,1)S(1)} collective-permute-done((f16[2,256,256]{2,1,0:T(8,128)(2,1)S(1)}, f16[2,256,256]{2,1,0:T(8,128)(2,1)S(1)}, u32[]{:S(2)}, u32[]{:S(2)}) %collective-permute-start.22) | collective-permute-done | bytes 262176 | tf_op jit(solution)/shard_map/ppermute | solution.py:463
  211.8 1.5 collective-permute-start.17
  213.2 1.1 fusion.16
  215.1 1.5 collective-permute-start.19
  217.4 1.5 collective-permute-start.20
  219.9 2.3 fusion.10
  222.1 27.2 %collective-permute-done.17.refs_8_ = bf16[2,256,512]{2,1,0:T(8,128)(2,1)} collective-permute-done((bf16[2,256,512]{2,1,0:T(8,128)(2,1)}, bf16[2,256,512]{2,1,0:T(8,128)(2,1)}, u32[]{:S(2)}, u32[]{:S(2)}) %collective-permute-start.17) | collective-permute-done | bytes 524320 | tf_op jit(solution)/shard_map/ppermute | solution.py:258
  249.3 8.2 %collective-permute-done.18.refs_9_ = bf16[2,256,512]{2,1,0:T(8,128)(2,1)} collective-permute-done((bf16[2,256,512]{2,1,0:T(8,128)(2,1)}, bf16[2,256,512]{2,1,0:T(8,128)(2,1)}, u32[]{:S(2)}, u32[]{:S(2)}) %collective-permute-start.18) | collective-permute-done | bytes 524320 | tf_op jit(solution)/shard_map/ppermute | solution.py:258
  257.6 11.2 %hartree.1 = bf16[512,1024]{1,0:T(8,128)(2,1)} custom-call(s32[8]{0:T(128)} %copy-done.17, s32[2,4]{1,0:T(2,128)} %refs_1_.1, f32[2,4096]{1,0:T(2,128)} %bitcast.122, bf16[1024,4096]{1,0:T(8,128)(2,1)} %bitcast.121, bf16[2,256,512]{2,1,0:T(8,128)(2,1)} %get-tuple-element.22.refs_4_, bf16[2,256,512]{2,1,0:T(8,128)(2,1)} %copy-done.21, ...), custom_call_target="tpu_custom_call" | custom-call | flops 4294967296 | bytes 12582912 | tf_op jit(solution)/shard_map/hartree/pallas_call | solution.py:221
  (132 shorter events, 20.2 us)
Async XLA Ops:
  0.6 10.3 %copy-start = (f32[32,64,256]{2,1,0:T(8,128)S(1)}, f32[32,64,256]{2,1,0:T(8,128)}, u32[]{:S(2)}) copy-start(f32[32,64,256]{2,1,0:T(8,128)} %param.19) | copy-start | bytes 6291460
  2.1 8.9 %copy-start.5 = (f32[256,256]{1,0:T(8,128)S(1)}, f32[256,256]{1,0:T(8,128)}, u32[]{:S(2)}) copy-start(f32[256,256]{1,0:T(8,128)} %constant.119.clone) | copy-start | bytes 786436
  3.5 32.1 %collective-permute-start.4 = (bf16[512,1024]{1,0:T(8,128)(2,1)}, bf16[512,1024]{1,0:T(8,128)(2,1)}, u32[]{:S(2)}, u32[]{:S(2)}) collective-permute-start(bf16[512,1024]{1,0:T(8,128)(2,1)} %mul.148.refs_3_), channel_id=1, source_target_pairs={{0,8},{1,9},{2,10},{3,11},{4,12},{5,13},{6,14},{7,15},{8,0},{9,1},... | collective-permute-start | bytes 3145736 | tf_op jit(solution)/shard_map/ppermute | solution.py:258
  6.5 37.8 %collective-permute-start.9 = (bf16[512,1024]{1,0:T(8,128)(2,1)}, bf16[512,1024]{1,0:T(8,128)(2,1)}, u32[]{:S(2)}, u32[]{:S(2)}) collective-permute-start(bf16[512,1024]{1,0:T(8,128)(2,1)} %mul.148.refs_3_), channel_id=1, source_target_pairs={{0,4},{1,5},{2,6},{3,7},{4,0},{5,1},{6,2},{7,3},{8,12},{9,13},{10,... | collective-permute-start | bytes 3145736 | tf_op jit(solution)/shard_map/ppermute | solution.py:258
  6.5 32.5 %collective-permute-start.2 = (bf16[512,1024]{1,0:T(8,128)(2,1)}, bf16[512,1024]{1,0:T(8,128)(2,1)}, u32[]{:S(2)}, u32[]{:S(2)}) collective-permute-start(bf16[512,1024]{1,0:T(8,128)(2,1)} %mul.148.refs_3_), channel_id=1, source_target_pairs={{0,16},{1,17},{2,18},{3,19},{4,20},{5,21},{6,22},{7,23},{8,24},{9,... | collective-permute-start | bytes 3145736 | tf_op jit(solution)/shard_map/ppermute | solution.py:258
  9.3 3.8 %copy-start.2 = (bf16[4,256,512]{2,1,0:T(8,128)(2,1)}, bf16[4,256,512]{2,1,0:T(8,128)(2,1)S(1)}, u32[]{:S(2)}) copy-start(bf16[4,256,512]{2,1,0:T(8,128)(2,1)S(1)} %constant_dynamic-slice_fusion.1.refs_4_) | copy-start | bytes 3145732
  9.3 26.2 %collective-permute-start = (bf16[4,256,512]{2,1,0:T(8,128)(2,1)S(1)}, bf16[4,256,512]{2,1,0:T(8,128)(2,1)}, u32[]{:S(2)}, u32[]{:S(2)}) collective-permute-start(bf16[4,256,512]{2,1,0:T(8,128)(2,1)S(1)} %constant_dynamic-slice_fusion.1.refs_4_), channel_id=1, source_target_pairs={{0,1},{1,0},{2,3},{3,2},{4,5},{5,4},{6,7},{7,6},{8,9},{9,8},{10,11... | collective-permute-start | bytes 3145736 | tf_op jit(solution)/shard_map/ppermute | solution.py:290
  10.9 33.4 %collective-permute-start.1 = (bf16[4,256,512]{2,1,0:T(8,128)(2,1)S(1)}, bf16[4,256,512]{2,1,0:T(8,128)(2,1)}, u32[]{:S(2)}, u32[]{:S(2)}) collective-permute-start(bf16[4,256,512]{2,1,0:T(8,128)(2,1)S(1)} %constant_dynamic-slice_fusion.1.refs_4_), channel_id=1, source_target_pairs={{0,4},{1,2},{2,1},{3,7},{4,0},{5,6},{6,5},{7,3},{8,12},{9,10},{10,... | collective-permute-start | bytes 3145736 | tf_op jit(solution)/shard_map/ppermute | solution.py:290
  10.9 6.0 %copy-start.23 = (s32[4,1]{0,1:T(1,128)S(1)}, s32[4,1]{0,1:T(1,128)}, u32[]{:S(2)}) copy-start(s32[4,1]{0,1:T(1,128)} %param.16) | copy-start | bytes 52
  10.9 6.0 %copy-start.18 = (f32[3]{0:T(128)S(1)}, f32[3]{0:T(128)}, u32[]{:S(2)}) copy-start(f32[3]{0:T(128)} %param.21) | copy-start | bytes 40
  11.0 6.6 %copy-start.24 = (s32[16]{0:T(128)S(1)}, s32[16]{0:T(128)}, u32[]{:S(2)}) copy-start(s32[16]{0:T(128)} %param.20) | copy-start | bytes 196
  13.1 28.3 %copy-start.10 = (bf16[1024,256]{1,0:T(8,128)(2,1)S(1)}, bf16[1024,256]{1,0:T(8,128)(2,1)}, u32[]{:S(2)}) copy-start(bf16[1024,256]{1,0:T(8,128)(2,1)} %param.15) | copy-start | bytes 1572868
  13.1 44.8 %all-to-all-start = ((f16[32,8,2048]{2,1,0:T(8,128)(2,1)}), f16[32,8,2048]{2,1,0:T(8,128)(2,1)}, u32[]{:S(2)}, u32[]{:S(2)}) async-start(f16[32,8,2048]{2,1,0:T(8,128)(2,1)} %fusion.1), calls=%async_computation | async-start | bytes 2097152 | tf_op jit(solution)/shard_map/all_to_all | solution.py:30
  19.0 25.4 %copy-start.17 = (s32[8]{0:T(128)}, s32[8]{0:T(128)S(1)}, u32[]{:S(2)}) copy-start(s32[8]{0:T(128)S(1)} %iota_xor_fusion.refs_0_) | copy-start | bytes 100
  35.5 36.0 %collective-permute-start.12 = (bf16[4,256,512]{2,1,0:T(8,128)(2,1)}, bf16[4,256,512]{2,1,0:T(8,128)(2,1)}, u32[]{:S(2)}, u32[]{:S(2)}) collective-permute-start(bf16[4,256,512]{2,1,0:T(8,128)(2,1)} %collective-permute-done.refs_5_), channel_id=1, source_target_pairs={{0,4},{1,2},{2,1},{3,7},{4,0},{5,6},{6,5},{7,3},{8,12},{9,10},{10,... | collective-permute-start | bytes 3145736 | tf_op jit(solution)/shard_map/ppermute | solution.py:290
  35.6 47.9 %collective-permute-start.10 = (bf16[512,1024]{1,0:T(8,128)(2,1)}, bf16[512,1024]{1,0:T(8,128)(2,1)}, u32[]{:S(2)}, u32[]{:S(2)}) collective-permute-start(bf16[512,1024]{1,0:T(8,128)(2,1)} %collective-permute-done.4.refs_5_), channel_id=1, source_target_pairs={{0,4},{1,5},{2,6},{3,7},{4,0},{5,1},{6,2},{7,3},{8,12},{9,13},{10,... | collective-permute-start | bytes 3145736 | tf_op jit(solution)/shard_map/ppermute | solution.py:258
  38.9 30.2 %collective-permute-start.5 = (bf16[256,1024]{1,0:T(8,128)(2,1)}, bf16[256,1024]{1,0:T(8,128)(2,1)}, u32[]{:S(2)}, u32[]{:S(2)}) collective-permute-start(bf16[256,1024]{1,0:T(8,128)(2,1)} %slice.46), channel_id=1, source_target_pairs={{0,16},{1,17},{2,18},{3,19},{4,20},{5,21},{6,22},{7,23},{8,24},{9,... | collective-permute-start | bytes 1572872 | tf_op jit(solution)/shard_map/ppermute | solution.py:258
  44.3 39.2 %collective-permute-start.6 = (bf16[256,1024]{1,0:T(8,128)(2,1)}, bf16[256,1024]{1,0:T(8,128)(2,1)}, u32[]{:S(2)}, u32[]{:S(2)}) collective-permute-start(bf16[256,1024]{1,0:T(8,128)(2,1)} %slice.47), channel_id=1, source_target_pairs={{0,8},{1,9},{2,10},{3,11},{4,12},{5,13},{6,14},{7,15},{8,0},{9,1},... | collective-permute-start | bytes 1572872 | tf_op jit(solution)/shard_map/ppermute | solution.py:258
  44.4 51.6 %collective-permute-start.3 = (bf16[512,1024]{1,0:T(8,128)(2,1)}, bf16[512,1024]{1,0:T(8,128)(2,1)}, u32[]{:S(2)}, u32[]{:S(2)}) collective-permute-start(bf16[512,1024]{1,0:T(8,128)(2,1)} %collective-permute-done.2.refs_3_), channel_id=1, source_target_pairs={{0,4},{1,5},{2,6},{3,7},{4,0},{5,1},{6,2},{7,3},{8,12},{9,13},{10,... | collective-permute-start | bytes 3145736 | tf_op jit(solution)/shard_map/ppermute | solution.py:258
  65.3 17.1 %copy-start.4 = (f32[256,256,1]{1,0,2:T(8,128)S(1)}, f32[256,256,1]{1,0,2:T(8,128)}, u32[]{:S(2)}) copy-start(f32[256,256,1]{1,0,2:T(8,128)} %constant.126) | copy-start | bytes 786436
  69.1 14.9 %copy-start.11 = (f32[256,256,1]{1,0,2:T(8,128)S(1)}, f32[256,256,1]{1,0,2:T(8,128)}, u32[]{:S(2)}) copy-start(f32[256,256,1]{1,0,2:T(8,128)} %constant.127) | copy-start | bytes 786436
  69.2 37.5 %collective-permute-start.11 = (bf16[4,256,512]{2,1,0:T(8,128)(2,1)}, bf16[4,256,512]{2,1,0:T(8,128)(2,1)}, u32[]{:S(2)}, u32[]{:S(2)}) collective-permute-start(bf16[4,256,512]{2,1,0:T(8,128)(2,1)} %collective-permute-done.1.refs_6_), channel_id=1, source_target_pairs={{0,1},{1,0},{2,3},{3,2},{4,5},{5,4},{6,7},{7,6},{8,9},{9,8},{10,11... | collective-permute-start | bytes 3145736 | tf_op jit(solution)/shard_map/ppermute | solution.py:290
  71.5 46.8 %collective-permute-start.13 = (bf16[4,256,512]{2,1,0:T(8,128)(2,1)}, bf16[4,256,512]{2,1,0:T(8,128)(2,1)}, u32[]{:S(2)}, u32[]{:S(2)}) collective-permute-start(bf16[4,256,512]{2,1,0:T(8,128)(2,1)} %collective-permute-done.12.refs_8_), channel_id=1, source_target_pairs={{0,1},{1,0},{2,3},{3,2},{4,5},{5,4},{6,7},{7,6},{8,9},{9,8},{10,11... | collective-permute-start | bytes 3145736 | tf_op jit(solution)/shard_map/ppermute | solution.py:290
  83.4 12.6 %collective-permute-start.7 = (bf16[256,1024]{1,0:T(8,128)(2,1)}, bf16[256,1024]{1,0:T(8,128)(2,1)S(1)}, u32[]{:S(2)}, u32[]{:S(2)}) collective-permute-start(bf16[256,1024]{1,0:T(8,128)(2,1)} %collective-permute-done.5.refs_5_), channel_id=1, source_target_pairs={{0,4},{1,5},{2,6},{3,7},{4,0},{5,1},{6,2},{7,3},{8,12},{9,13},{10,... | collective-permute-start | bytes 1572872 | tf_op jit(solution)/shard_map/ppermute | solution.py:258
  83.5 12.5 %collective-permute-start.8 = (bf16[256,1024]{1,0:T(8,128)(2,1)}, bf16[256,1024]{1,0:T(8,128)(2,1)S(1)}, u32[]{:S(2)}, u32[]{:S(2)}) collective-permute-start(bf16[256,1024]{1,0:T(8,128)(2,1)} %collective-permute-done.6.refs_6_), channel_id=1, source_target_pairs={{0,4},{1,5},{2,6},{3,7},{4,0},{5,1},{6,2},{7,3},{8,12},{9,13},{10,... | collective-permute-start | bytes 1572872 | tf_op jit(solution)/shard_map/ppermute | solution.py:258
  118.3 11.1 %copy-start.14 = (f32[128,256]{1,0:T(8,128)S(1)}, f32[128,256]{1,0:T(8,128)}, u32[]{:S(2)}) copy-start(f32[128,256]{1,0:T(8,128)} %constant.117.clone) | copy-start | bytes 393220
  118.3 16.5 %copy-start.3 = (f32[8,256,256]{2,1,0:T(8,128)S(1)}, f32[8,256,256]{2,1,0:T(8,128)}, u32[]{:S(2)}) copy-start(f32[8,256,256]{2,1,0:T(8,128)} %get-tuple-element.30) | copy-start | bytes 6291460
  130.5 11.6 %all-to-all-start.1 = ((f32[32,1,512]{2,1,0:T(1,128)}), f32[32,1,512]{2,1,0:T(1,128)S(1)}, u32[]{:S(2)}, u32[]{:S(2)}) async-start(f32[32,1,512]{2,1,0:T(1,128)} %reshape.373), calls=%async_computation.1 | async-start | bytes 131072 | tf_op jit(solution)/shard_map/all_to_all | solution.py:30
  136.0 12.0 %copy-start.16 = (f32[32,256,1]{1,0,2:T(8,128)S(1)}, f32[32,256,1]{1,0,2:T(8,128)}, u32[]{:S(2)}) copy-start(f32[32,256,1]{1,0,2:T(8,128)} %constant.128) | copy-start | bytes 98308
  136.0 12.3 %copy-start.12 = (f32[256,256]{0,1:T(8,128)S(1)}, f32[256,256]{0,1:T(8,128)}, u32[]{:S(2)}) copy-start(f32[256,256]{0,1:T(8,128)} %broadcast_add_fusion) | copy-start | bytes 786436
  142.1 21.2 %all-to-all-start.3 = ((f16[8,256,256]{2,1,0:T(8,128)(2,1)}), f16[8,256,256]{2,1,0:T(8,128)(2,1)}, u32[]{:S(2)}, u32[]{:S(2)}) async-start(f16[8,256,256]{2,1,0:T(8,128)(2,1)} %multiply_convert_fusion), calls=%async_computation.3 | async-start | bytes 2097152 | tf_op jit(solution)/shard_map/all_to_all | solution.py:457
  163.3 11.2 %copy-start.25 = (s32[1,2]{1,0:T(1,128)S(1)}, s32[1,2]{1,0:T(1,128)}, u32[]{:S(2)}) copy-start(s32[1,2]{1,0:T(1,128)} %param.17) | copy-start | bytes 28
  163.3 55.6 %all-to-all-start.2 = ((bf16[32,8,2176]{2,1,0:T(8,128)(2,1)}), bf16[32,8,2176]{2,1,0:T(8,128)(2,1)S(1)}, u32[]{:S(2)}, u32[]{:S(2)}) async-start(bf16[32,8,2176]{2,1,0:T(8,128)(2,1)} %pad_maximum_fusion), calls=%async_computation.2 | async-start | bytes 2228224 | tf_op jit(solution)/shard_map/all_to_all | solution.py:30
  167.0 48.1 %copy-start.20 = (bf16[2,256,512]{2,1,0:T(8,128)(2,1)S(1)}, bf16[2,256,512]{2,1,0:T(8,128)(2,1)}, u32[]{:S(2)}) copy-start(bf16[2,256,512]{2,1,0:T(8,128)(2,1)} %get-tuple-element.28) | copy-start | bytes 1572868
  167.0 50.4 %copy-start.19 = (bf16[2,256,512]{2,1,0:T(8,128)(2,1)S(1)}, bf16[2,256,512]{2,1,0:T(8,128)(2,1)}, u32[]{:S(2)}) copy-start(bf16[2,256,512]{2,1,0:T(8,128)(2,1)} %get-tuple-element.29) | copy-start | bytes 1572868
  167.0 52.0 %copy-start.13 = (f32[128,256,1]{1,0,2:T(8,128)S(1)}, f32[128,256,1]{1,0,2:T(8,128)}, u32[]{:S(2)}) copy-start(f32[128,256,1]{1,0,2:T(8,128)} %constant.130) | copy-start | bytes 393220
  167.0 52.9 %copy-start.6 = (f32[256,256]{1,0:T(8,128)S(1)}, f32[256,256]{1,0:T(8,128)}, u32[]{:S(2)}) copy-start(f32[256,256]{1,0:T(8,128)} %constant.119.clone) | copy-start | bytes 786436
  167.0 48.1 %collective-permute-start.14 = (bf16[2,256,512]{2,1,0:T(8,128)(2,1)}, bf16[2,256,512]{2,1,0:T(8,128)(2,1)S(1)}, u32[]{:S(2)}, u32[]{:S(2)}) collective-permute-start(bf16[2,256,512]{2,1,0:T(8,128)(2,1)} %get-tuple-element.23), channel_id=1, source_target_pairs={{0,4},{1,5},{2,6},{3,7},{4,0},{5,1},{6,2},{7,3},{8,12},{9,13},{10,... | collective-permute-start | bytes 1572872 | tf_op jit(solution)/shard_map/ppermute | solution.py:258
  167.1 49.5 %collective-permute-start.15 = (bf16[2,256,512]{2,1,0:T(8,128)(2,1)}, bf16[2,256,512]{2,1,0:T(8,128)(2,1)S(1)}, u32[]{:S(2)}, u32[]{:S(2)}) collective-permute-start(bf16[2,256,512]{2,1,0:T(8,128)(2,1)} %get-tuple-element.24), channel_id=1, source_target_pairs={{0,8},{1,9},{2,10},{3,11},{4,12},{5,13},{6,14},{7,15},{8,0},{9,1},... | collective-permute-start | bytes 1572872 | tf_op jit(solution)/shard_map/ppermute | solution.py:258
  170.0 22.0 %collective-permute-start.21 = (f16[2,256,256]{2,1,0:T(8,128)(2,1)S(1)}, f16[2,256,256]{2,1,0:T(8,128)(2,1)S(1)}, u32[]{:S(2)}, u32[]{:S(2)}) collective-permute-start(f16[2,256,256]{2,1,0:T(8,128)(2,1)S(1)} %get-tuple-element.31), channel_id=1, source_target_pairs={{0,1},{1,0},{2,3},{3,2},{4,5},{5,4},{6,7},{7,6},{8,9},{9,8},{10,11... | collective-permute-start | bytes 786440 | tf_op jit(solution)/shard_map/ppermute | solution.py:463
  171.5 40.2 %collective-permute-start.22 = (f16[2,256,256]{2,1,0:T(8,128)(2,1)S(1)}, f16[2,256,256]{2,1,0:T(8,128)(2,1)S(1)}, u32[]{:S(2)}, u32[]{:S(2)}) collective-permute-start(f16[2,256,256]{2,1,0:T(8,128)(2,1)S(1)} %get-tuple-element.33), channel_id=1, source_target_pairs={{0,2},{1,3},{2,0},{3,1},{4,6},{5,7},{6,4},{7,5},{8,10},{9,11},{10,... | collective-permute-start | bytes 786440 | tf_op jit(solution)/shard_map/ppermute | solution.py:463
  174.0 39.3 %collective-permute-start.23 = (f16[2,256,256]{2,1,0:T(8,128)(2,1)S(1)}, f16[2,256,256]{2,1,0:T(8,128)(2,1)S(1)}, u32[]{:S(2)}, u32[]{:S(2)}) collective-permute-start(f16[2,256,256]{2,1,0:T(8,128)(2,1)S(1)} %get-tuple-element.32), channel_id=1, source_target_pairs={{0,3},{1,2},{2,1},{3,0},{4,7},{5,6},{6,5},{7,4},{8,11},{9,10},{10,... | collective-permute-start | bytes 786440 | tf_op jit(solution)/shard_map/ppermute | solution.py:463
  192.0 30.2 %collective-permute-start.16 = (bf16[2,256,512]{2,1,0:T(8,128)(2,1)}, bf16[2,256,512]{2,1,0:T(8,128)(2,1)}, u32[]{:S(2)}, u32[]{:S(2)}) collective-permute-start(bf16[2,256,512]{2,1,0:T(8,128)(2,1)} %get-tuple-element.25), channel_id=1, source_target_pairs={{0,12},{1,13},{2,14},{3,15},{4,8},{5,9},{6,10},{7,11},{8,4},{9,5},... | collective-permute-start | bytes 1572872 | tf_op jit(solution)/shard_map/ppermute | solution.py:258
  211.8 37.6 %collective-permute-start.17 = (bf16[2,256,512]{2,1,0:T(8,128)(2,1)}, bf16[2,256,512]{2,1,0:T(8,128)(2,1)}, u32[]{:S(2)}, u32[]{:S(2)}) collective-permute-start(bf16[2,256,512]{2,1,0:T(8,128)(2,1)} %get-tuple-element.26), channel_id=1, source_target_pairs={{0,16},{1,17},{2,18},{3,19},{4,20},{5,21},{6,22},{7,23},{8,24},{9,... | collective-permute-start | bytes 1572872 | tf_op jit(solution)/shard_map/ppermute | solution.py:258
  213.2 44.3 %collective-permute-start.18 = (bf16[2,256,512]{2,1,0:T(8,128)(2,1)}, bf16[2,256,512]{2,1,0:T(8,128)(2,1)}, u32[]{:S(2)}, u32[]{:S(2)}) collective-permute-start(bf16[2,256,512]{2,1,0:T(8,128)(2,1)} %get-tuple-element.27), channel_id=1, source_target_pairs={{0,20},{1,21},{2,22},{3,23},{4,16},{5,17},{6,18},{7,19},{8,28},{9,... | collective-permute-start | bytes 1572872 | tf_op jit(solution)/shard_map/ppermute | solution.py:258
  215.1 42.5 %collective-permute-start.19 = (bf16[2,256,512]{2,1,0:T(8,128)(2,1)S(1)}, bf16[2,256,512]{2,1,0:T(8,128)(2,1)}, u32[]{:S(2)}, u32[]{:S(2)}) collective-permute-start(bf16[2,256,512]{2,1,0:T(8,128)(2,1)S(1)} %copy-done.20), channel_id=1, source_target_pairs={{0,24},{1,25},{2,26},{3,27},{4,28},{5,29},{6,30},{7,31},{8,16},{9,... | collective-permute-start | bytes 1572872 | tf_op jit(solution)/shard_map/ppermute | solution.py:258
  217.4 40.1 %collective-permute-start.20 = (bf16[2,256,512]{2,1,0:T(8,128)(2,1)S(1)}, bf16[2,256,512]{2,1,0:T(8,128)(2,1)}, u32[]{:S(2)}, u32[]{:S(2)}) collective-permute-start(bf16[2,256,512]{2,1,0:T(8,128)(2,1)S(1)} %copy-done.19), channel_id=1, source_target_pairs={{0,28},{1,29},{2,30},{3,31},{4,24},{5,25},{6,26},{7,27},{8,20},{9,... | collective-permute-start | bytes 1572872 | tf_op jit(solution)/shard_map/ppermute | solution.py:258
  257.6 11.3 %copy-start.1 = (f32[32,64,256]{2,1,0:T(8,128)S(1)}, f32[32,64,256]{2,1,0:T(8,128)}, u32[]{:S(2)}) copy-start(f32[32,64,256]{2,1,0:T(8,128)} %param.19) | copy-start | bytes 6291460
  (6 other events, 9.0 us)

commit v3 on v2

--- a/solution.py
+++ b/solution.py
@@ -44,34 +44,47 @@
     return jnp.where(at_anchor, 0.0, 4.0 * math.pi / jnp.where(at_anchor, 1.0, squared))
 
 
-def after(values, *others):
-    return lax.optimization_barrier((values,) + others)[0]
-
-
 def lift_kernel(order_ref, basis_ref, margin_ref, *refs, places, held_before):
     part_refs = refs[: len(places)]
-    lifted_ref, window_ref, held = refs[len(places) + held_before :]
+    lifted_ref, window_ref, held, sems = refs[len(places) + held_before :]
     step = pl.program_id(0)
-    for part_ref, (e, start) in zip(part_refs, places):
+
+    def copies(e):
+        return [
+            pltpu.make_async_copy(
+                part_ref, held.at[e, pl.ds(start, part_ref.shape[0])], sems.at[i]
+            )
+            for i, (part_ref, (owner, start)) in enumerate(zip(part_refs, places))
+            if owner == e
+        ]
+
+    @pl.when(step == 0)
+    def _():
+        for e in range(held.shape[0]):
+            for copy in copies(e):
+                copy.start()
+
+    for e in range(held.shape[0]):
 
         @pl.when(step == e)
-        def _(part_ref=part_ref, start=start):
-            held[start : start + part_ref.shape[0], :] = part_ref[...]
+        def _(e=e):
+            for copy in copies(e):
+                copy.wait()
 
     block = margin_ref.shape[1]
     window_ref[0] = jnp.dot(
-        held[:block, :], margin_ref[...], preferred_element_type=jnp.float32
-    )
-
-    @pl.loop(0, held.shape[0] // block)
+        held[step, :block, :], margin_ref[...], preferred_element_type=jnp.float32
+    )
+
+    @pl.loop(0, held.shape[1] // block)
     def _(i):
         at = pl.ds(pl.multiple_of(i * block, block), block)
         lifted_ref[0, at, :] = jnp.dot(
-            held[at, :], basis_ref[...], preferred_element_type=jnp.float32
-        )
-
-
-def lift(order, basis, margin, parts, total, before=()):
+            held[step, at, :], basis_ref[...], preferred_element_type=jnp.float32
+        )
+
+
+def lift(order, basis, margin, parts, total, first, before=()):
     count = order.shape[0]
     pieces = [piece for part in parts for piece in part]
     places = []
@@ -98,13 +111,15 @@
                 pl.BlockSpec((depth, width), whole, pipeline_mode=once),
                 pl.BlockSpec((depth, block), whole, pipeline_mode=once),
             ]
-            + [pl.BlockSpec(piece.shape, whole, pipeline_mode=once) for piece in pieces]
-            + [pl.BlockSpec(memory_space=pl.ANY) for _ in before],
+            + [pl.BlockSpec(memory_space=pl.ANY) for _ in pieces + list(before)],
             out_specs=[
                 pl.BlockSpec((1, height, width), lambda i, s: (s[i], 0, 0)),
-                pl.BlockSpec((1, block, block), lambda i, s: (s[i], 0, 0)),
+                pl.BlockSpec((1, block, block), lambda i, s: (first + i, 0, 0)),
             ],
-            scratch_shapes=[pltpu.VMEM((height, depth), jnp.bfloat16)],
+            scratch_shapes=[
+                pltpu.VMEM((count, height, depth), jnp.bfloat16),
+                pltpu.SemaphoreType.DMA((len(pieces),)),
+            ],
         ),
         input_output_aliases={first_before + i: i for i in range(len(before))},
         cost_estimate=pl.CostEstimate(
@@ -242,6 +257,145 @@
         ),
         name="hartree",
     )(slots, pattern, pot, columns, *row_parts)
+
+
+def split_table(table):
+    leading = table.astype(jnp.bfloat16)
+    return leading, (table - leading.astype(np.float32)).astype(jnp.bfloat16)
+
+
+def split_values(values):
+    leading = values.astype(jnp.bfloat16)
+    return leading, (values - leading.astype(jnp.float32)).astype(jnp.bfloat16)
+
+
+def dot_split(left_side, right_side):
+    dot = lambda a, b: jnp.dot(a, b, preferred_element_type=jnp.float32)
+    return (
+        dot(left_side[0], right_side[0])
+        + dot(left_side[0], right_side[1])
+        + dot(left_side[1], right_side[0])
+    )
+
+
+def merge_lanes(part_of, count, width, shift_of):
+    lane = lax.broadcasted_iota(jnp.int32, (1, 128), 1)
+    merged = None
+    for i in range(count):
+        shift = shift_of(i) * width % 128
+        part = part_of(i)
+        part = pltpu.roll(part, shift, 1) if shift else part
+        merged = part if merged is None else jnp.where(lane >= i * width, part, merged)
+    return merged
+
+
+def forward_kernel(values_ref, xh_ref, xl_ref, yh_ref, yl_ref, out_ref, *, clus, col, lines):
+    size = out_ref.shape[1]
+    fold = 128 // lines
+
+    def source(c):
+        return jnp.concatenate([values_ref[k * col + c, 0] for k in range(clus)], axis=0)
+
+    sources = [source(c) for c in range(col)]
+    plane = jnp.concatenate(
+        [
+            jnp.concatenate(
+                [
+                    merge_lanes(lambda s: sources[j * fold + s], fold, lines, lambda s: s - p)
+                    for j in range(size // 128)
+                ],
+                axis=1,
+            )
+            for p in range(fold)
+        ],
+        axis=0,
+    )
+    plane = dot_split(split_values(plane), (yh_ref[...], yl_ref[...]))
+    out_ref[0] = dot_split((xh_ref[...], xl_ref[...]), split_values(plane))
+
+
+def forward_planes(values, x_table, y_table, clus, col, lines):
+    devices, depth, tiles, lanes = values.shape
+    size = x_table[0].shape[0]
+    table = pl.BlockSpec((size, size), lambda i: (0, 0), pipeline_mode=pl.Buffered(1))
+    return pl.pallas_call(
+        lambda *refs: forward_kernel(*refs, clus=clus, col=col, lines=lines),
+        out_shape=jax.ShapeDtypeStruct((depth, size, size), jnp.float32),
+        grid=(depth,),
+        in_specs=[pl.BlockSpec((devices, 1, tiles, lanes), lambda i: (0, i, 0, 0))] + [table] * 4,
+        out_specs=pl.BlockSpec((1, size, size), lambda i: (i, 0, 0)),
+        cost_estimate=pl.CostEstimate(
+            flops=12 * depth * size**3, bytes_accessed=8 * depth * size**2, transcendentals=0
+        ),
+        name="forward",
+    )(values, *x_table, *y_table)
+
+
+def inverse_kernel(
+    plane_ref, factor_ref, patch_ref, spread_ref, pick_ref, lines_ref, *refs, clus, col, lines
+):
+    xh_ref, xl_ref, yh_ref, yl_ref, out_ref, held = refs
+    step = pl.program_id(0)
+    depth, tiles = held.shape[0], out_ref.shape[2]
+    fold = 128 // lines
+    exact = lambda a, b: jnp.dot(
+        a, b, precision=lax.Precision.HIGHEST, preferred_element_type=jnp.float32
+    )
+    plane = (plane_ref[0] + exact(spread_ref[...], patch_ref[0])) * factor_ref[0]
+    picked = None
+    for b in range(pick_ref.shape[0]):
+        value = exact(exact(pick_ref[b], plane), lines_ref[b])
+        picked = value if picked is None else picked + value
+    lane = lax.broadcasted_iota(jnp.int32, picked.shape, 1)
+    leading = picked.astype(jnp.bfloat16).astype(jnp.float32)
+    held[step] = jnp.where(lane < 64, picked, picked - leading)
+    plane = dot_split((xh_ref[...], xl_ref[...]), split_values(plane))
+    plane = dot_split(split_values(plane), (yh_ref[...], yl_ref[...]))
+    height = clus * tiles
+    for c in range(col):
+        at = c // fold * 128
+        merged = merge_lanes(
+            lambda p: plane[p * height : (p + 1) * height, at : at + 128],
+            fold,
+            lines,
+            lambda p: p - c % fold,
+        ).astype(jnp.bfloat16)
+        for k in range(clus):
+            out_ref[k * col + c, step] = merged[k * tiles : (k + 1) * tiles]
+
+    @pl.when(step == depth - 1)
+    def _():
+        for k in range(clus):
+            rows = jnp.concatenate(
+                [held[:, k, :], jnp.zeros((tiles - depth, 128), jnp.float32)], axis=0
+            ).astype(jnp.bfloat16)
+            for c in range(col):
+                out_ref[k * col + c, depth] = rows
+
+
+def inverse_planes(plane, factor, patch, spread, pick, line_table, x_table, y_table, tiles, clus, col, lines):
+    depth, size, _ = plane.shape
+    blocks = patch.shape[1]
+    devices = clus * col
+    once = pl.Buffered(1)
+    whole = lambda array: pl.BlockSpec(
+        array.shape, lambda i: (0,) * array.ndim, pipeline_mode=once
+    )
+    by_plane = pl.BlockSpec((1, size, size), lambda i: (i, 0, 0))
+    constants = (spread, pick, line_table, *x_table, *y_table)
+    return pl.pallas_call(
+        lambda *refs: inverse_kernel(*refs, clus=clus, col=col, lines=lines),
+        out_shape=jax.ShapeDtypeStruct((devices, depth + 1, tiles, 128), jnp.bfloat16),
+        grid=(depth,),
+        in_specs=[by_plane, by_plane, pl.BlockSpec((1, blocks, size), lambda i: (i, 0, 0))]
+        + [whole(array) for array in constants],
+        out_specs=pl.BlockSpec((devices, depth + 1, tiles, 128), lambda i: (0, 0, 0, 0)),
+        scratch_shapes=[pltpu.VMEM((depth, clus, 128), jnp.float32)],
+        cost_estimate=pl.CostEstimate(
+            flops=12 * depth * size**3, bytes_accessed=10 * depth * size**2, transcendentals=0
+        ),
+        name="inverse",
+    )(plane, factor, patch, *constants)
 
 
 def make_program(clus_count, col_count):
@@ -340,6 +494,24 @@
             + np.arange(groups)[:, None] * lines_dev
             + line_id[None, :] % lines_dev
         )
+        fold = 128 // lines
+        tiles = planes * lines // 128
+        pot_lanes = 2 * rows * patch_lines
+        in_kernels = tiles % 16 == 0 and tiles >= depth and groups == 1 and pot_lanes == 128
+        row_id = np.arange(size)
+        x_of_row = (
+            row_id // tiles % clus_count * planes
+            + row_id % tiles * fold
+            + row_id // (tiles * clus_count)
+        )
+        forward_x = split_table(hartley[:, x_of_row] * np.float32(1.0 / 256.0))
+        inverse_x = split_table(hartley[x_of_row])
+        both_y = split_table(hartley)
+        line_table = np.zeros((rows, size, pot_lanes), np.float32)
+        for b in range(rows):
+            for part in range(2):
+                start = (part * rows + b) * patch_lines
+                line_table[b, :, start : start + patch_lines] = hartley[y_cells[0]].T
         hartley_y = jnp.asarray(hartley[y_cells])
         hartley = jnp.asarray(hartley)
 
@@ -358,28 +530,35 @@
 
         rest_lines = rest_density.reshape(planes * lines, size)
         waves = dot_high("kz,lz->kl", hartley, rest_lines)
-        moved = exchange((waves * 256.0).astype(jnp.float16).reshape(devices, depth, planes * lines))
-        moved = after(moved, pieces[1], pieces[2])
-        plane = (
-            moved.reshape(clus_count, col_count, depth, planes, lines)
-            .transpose(2, 0, 3, 1, 4)
-            .reshape(depth, size, size)
-            .astype(jnp.float32)
-        )
-        plane = dot_high("axy,yv->axv", plane, hartley)
-        plane = dot_high("ux,axv->auv", hartley * (1.0 / 256.0), plane)
+        waves = (waves * 256.0).astype(jnp.float16)
+        if in_kernels:
+            waves = waves.reshape(devices, depth, tiles, 128)
+        else:
+            waves = waves.reshape(devices, depth, planes * lines)
+        moved = exchange(waves)
+        if in_kernels:
+            plane = forward_planes(
+                moved.astype(jnp.float32), forward_x, both_y, clus_count, col_count, lines
+            )
+        else:
+            plane = (
+                moved.reshape(clus_count, col_count, depth, planes, lines)
+                .transpose(2, 0, 3, 1, 4)
+                .reshape(depth, size, size)
+                .astype(jnp.float32)
+            )
+            plane = dot_high("axy,yv->axv", plane, hartley)
+            plane = dot_high("ux,axv->auv", hartley * (1.0 / 256.0), plane)
 
         phi_slice = own_phi.reshape(cols * block, slice_cells)
         margin_masked = (
             margin_window.reshape(cols, block, block)
             * ovl_pattern.astype(jnp.bfloat16)[:, :, None]
         ).reshape(cols * block, block)
-        split = clus_count // 2
-        before = lift(
-            clus_ids[:split], phi_slice, margin_masked, gathered[:split], clus_count
-        )
+        split = 2
+        before = lift(clus_ids[:split], phi_slice, margin_masked, gathered[:split], clus_count, 0)
         lifted, window = lift(
-            clus_ids[split:], phi_slice, margin_masked, gathered[split:], clus_count, before
+            clus_ids[split:], phi_slice, margin_masked, gathered[split:], clus_count, split, before
         )
         where = jnp.asarray(place)[c][clus_ids // ratio]
         *sent, partial_rho = route(clus_ids, where, clus_ids % ratio, lifted, pieces, rows)
@@ -397,8 +576,8 @@
         patch_sum = patch_sum.transpose(2, 3, 1, 0, 4).reshape(
             groups, group_size, depth, patch_lines
         )
-        patch_y = dot_high("gizm,gmv->gizv", patch_sum, hartley_y)
-        patch_y = patch_y.reshape(all_blocks, depth, size)
+        patch_y = dot_high("gizm,gmv->zgiv", patch_sum, hartley_y)
+        patch_y = patch_y.reshape(depth, all_blocks, size)
         block_ids = jnp.arange(all_blocks, dtype=jnp.int32)
         x_cells = slab_owner.astype(jnp.int32) * planes + block_ids % planes
         chosen = (x_cells[:, None] == jnp.arange(size, dtype=jnp.int32)[None, :]).astype(jnp.float32)
@@ -410,38 +589,54 @@
         for e, part in enumerate(sent):
             row_parts.append(part if e == 0 else swap(part, e))
 
-        plane = plane + dot_high("iu,izv->zuv", hartley_x, patch_y)
-
         factor = green_planes(cell_lengths, size, device_id * depth, depth) * (1.0 / size**3)
-        plane = plane * factor
-
-        picked = dot_high("iu,zuv->izv", hartley_x, plane).reshape(
-            groups, group_size, depth, size
-        )
-        picked = dot_high("gizv,gmv->gizm", picked, hartley_y).reshape(
-            clus_count, rows, depth, patch_lines
-        )
-        picked = picked.transpose(0, 2, 1, 3).reshape(clus_count, 1, depth, rows * patch_lines)
-        leading = lax.reduce_precision(picked, 8, 7)
-        picked = jnp.concatenate([leading, picked - leading], axis=-1).astype(jnp.bfloat16)
-        picked = jnp.broadcast_to(
-            picked, (clus_count, col_count, depth, 2 * rows * patch_lines)
-        ).reshape(devices, depth, 2 * rows * patch_lines)
-
-        plane = dot_high("xu,auv->axv", hartley, plane)
-        plane = dot_high("axv,vy->axy", plane, hartley)
-        back = (
-            plane.astype(jnp.bfloat16)
-            .reshape(depth, clus_count, planes, col_count, lines)
-            .transpose(1, 3, 0, 2, 4)
-            .reshape(devices, depth, planes * lines)
-        )
-        back = jnp.concatenate([back, picked], axis=-1)
-        back = exchange(back).reshape(size, planes * lines + 2 * rows * patch_lines)
-        picked = back[:, planes * lines :].astype(jnp.float32).reshape(size, 2, rows, patch_lines)
+
+        if in_kernels:
+            back = inverse_planes(
+                plane,
+                factor,
+                patch_y,
+                hartley_x.T,
+                hartley_x.reshape(clus_count, rows, size).transpose(1, 0, 2),
+                line_table,
+                inverse_x,
+                both_y,
+                tiles,
+                clus_count,
+                col_count,
+                lines,
+            )
+            back = exchange(back)
+            picked = back[:, depth, :depth]
+            back = back[:, :depth]
+        else:
+            plane = (plane + dot_high("iu,ziv->zuv", hartley_x, patch_y)) * factor
+            picked = dot_high("iu,zuv->izv", hartley_x, plane).reshape(
+                groups, group_size, depth, size
+            )
+            picked = dot_high("gizv,gmv->gizm", picked, hartley_y).reshape(
+                clus_count, rows, depth, patch_lines
+            )
+            picked = picked.transpose(0, 2, 1, 3).reshape(clus_count, 1, depth, rows * patch_lines)
+            leading = lax.reduce_precision(picked, 8, 7)
+            picked = jnp.concatenate([leading, picked - leading], axis=-1).astype(jnp.bfloat16)
+            picked = jnp.broadcast_to(picked, (clus_count, col_count, depth, pot_lanes))
+            picked = picked.reshape(devices, depth, pot_lanes)
+            plane = dot_high("xu,auv->axv", hartley, plane)
+            plane = dot_high("axv,vy->axy", plane, hartley)
+            back = (
+                plane.astype(jnp.bfloat16)
+                .reshape(depth, clus_count, planes, col_count, lines)
+                .transpose(1, 3, 0, 2, 4)
+                .reshape(devices, depth, planes * lines)
+            )
+            back = exchange(jnp.concatenate([back, picked], axis=-1))
+            picked = back[:, :, planes * lines :]
+            back = back[:, :, : planes * lines]
+        picked = picked.astype(jnp.float32).reshape(size, 2, rows, patch_lines)
         patch_pot = dot_high("krm,qk->rmq", picked[:, 0] + picked[:, 1], hartley_q)
         patch_pot = patch_pot.reshape(rows, cells)
-        back = back[:, : planes * lines].astype(jnp.float32)
+        back = back.reshape(size, planes * lines).astype(jnp.float32)
         potential = dot_high("kl,kz->lz", back, hartley).reshape(planes, lines, size)
 
         hartree = hartree_product(
@@ -454,8 +649,13 @@
 
         span = clus_count // col_count
         window = (window * 32.0).astype(jnp.float16)
-        window = lax.all_to_all(window, "clus", split_axis=0, concat_axis=0, tiled=True)
-        window = window.reshape(col_count, span, block, block)
+        arrived = []
+        for e in range(clus_count):
+            arrived.append(swap(window[e], e) if e else window[e])
+        arrived = jnp.stack(arrived)
+        window = jnp.stack(
+            [lax.dynamic_index_in_dim(arrived, k ^ b, 0, keepdims=False) for b in range(clus_count)]
+        ).reshape(col_count, span, block, block)
         summed = 0.0
         for step in range(col_count):
             part = lax.dynamic_index_in_dim(window, c ^ step, 0, keepdims=False)

time: 270 us -> 279 us (1.033); the launches traced: 269 us -> 274 us
  Pallas kernels: 40.9 us -> 66.1 us
  matrix products: 16.1 us -> 4.89 us
  local copies, waits for them, and re-layouts: 33.5 us -> 23.1 us
    ppermute x16 -> x23, waiting for transfers between devices: 35.5 us -> 66.6 us  [swap(): return lax.ppermute(values, AXES, pairs(lambda k, c: (k ^ distance, c)))]
    pallas_call x0 -> x2, Pallas kernels: none -> 25.9 us  [the longest x1 17.1 us: inverse_planes(): pl.pallas_call(lambda *refs: inverse_kernel(*refs, clus=clus, col=col, li...]
    ppermute x5, waiting for transfers between devices: 26.8 us -> 5.41 us  [gather_line(): arrays.append(lax.ppermute(arrays[source], AXES, moved))]
    reshape x7 -> x2, local copies, waits for them, and re-layouts: 13.5 us -> 0.61 us  [per_device(): hartley_x.reshape(clus_count, rows, size).transpose(1, 0, 2)]
    all_to_all x3, waiting for transfers between devices: 18.9 us -> 7.46 us  [exchange(): return lax.all_to_all(values, AXES, split_axis=0, concat_axis=0, tiled=True)]
    dot_general x12 -> x5, matrix products: 15.9 us -> 4.72 us  [dot_high(): jnp.einsum(equation, left_side, right_side, precision=HIGH, preferred_ele...]
    ppermute x16 -> x23, starting transfers between devices: 12.8 us -> 19.5 us  [swap(): return lax.ppermute(values, AXES, pairs(lambda k, c: (k ^ distance, c)))]
    all_to_all x1 -> x0, starting transfers between devices: 4.25 us -> none  [per_device(): lax.all_to_all(window, 'clus', split_axis=0, concat_axis=0, tiled=True)]
  transfers between devices with their start and end apart: 28 -> 34, of which waited for: 8 -> 11; matrix products, arithmetic and copies ran while one was open for 20% -> 13% of each run, Pallas kernels for 7% -> 20%
where the time goes in v3:
time: 279 us; the launch traced here: 274 us
  waiting for transfers between devices  117 us (42%)
  Pallas kernels  66.1 us (24%)
  starting transfers between devices  49 us (18%)
  local copies, waits for them, and re-layouts  23.1 us (8%)
  other arithmetic  12.5 us (4%)
  matrix products  4.89 us (2%)
    ppermute x23, waiting for transfers between devices, swap(): return lax.ppermute(values, AXES, pairs(lambda k, c: (k ^ distance, c)))  66.6 us
    ppermute x3, waiting for transfers between devices, per_device(): part = lax.ppermute(part, AXES, pairs(lambda k, c: (k, c ^ step)))  37.5 us
    ppermute x23, starting transfers between devices, swap(): return lax.ppermute(values, AXES, pairs(lambda k, c: (k ^ distance, c)))  19.5 us
    pallas_call x2, Pallas kernels, lift(): pl.pallas_call(lambda *refs: lift_kernel(*refs, places=places, held_befor...  18.5 us
    pallas_call x1, Pallas kernels, inverse_planes(): pl.pallas_call(lambda *refs: inverse_kernel(*refs, clus=clus, col=col, li...  17.1 us
    ppermute x5, starting transfers between devices, gather_line(): arrays.append(lax.ppermute(arrays[source], AXES, moved))  14.6 us
    pallas_call x1, Pallas kernels, hartree_product(): pl.pallas_call(lambda *refs: hartree_kernel(*refs, count=count), out_shap...  11.2 us
    all_to_all x3, starting transfers between devices, exchange(): return lax.all_to_all(values, AXES, split_axis=0, concat_axis=0, tiled=True)  10.5 us
  transfers between devices with their start and end apart: 34, of which 11 were waited for; matrix products, arithmetic and copies ran while one was open for 13% of the time, Pallas kernels for 20%

profile of v3, /device:TPU:0, one launch (start us, length us, event | category | flops | bytes accessed | tf_op | source)
XLA Modules:
  0.0 273.7 jit_solution(2775934670946342786)
XLA Ops:
  2.1 1.4 mul.147.refs_3_
  4.0 2.5 collective-permute-start
  6.4 1.5 collective-permute-start.2
  8.0 1.3 constant_dynamic-slice_fusion.refs_4_
  9.3 1.6 collective-permute-start.9
  10.9 1.1 fusion.3
  12.1 1.3 copy.71
  13.4 3.5 %all-to-all-start = ((f16[32,8,16,128]{3,2,1,0:T(8,128)(2,1)}), f16[32,8,16,128]{3,2,1,0:T(8,128)(2,1)S(1)}, u32[]{:S(2)}, u32[]{:S(2)}) async-start(f16[32,8,16,128]{3,2,1,0:T(8,128)(2,1)} %bitcast.117), calls=%async_computation | async-start | bytes 2097152 | tf_op jit(solution)/shard_map/all_to_all | solution.py:30
  17.7 1.3 divide_multiply_fusion
  19.9 10.9 %collective-permute-done.refs_3_ = bf16[512,1024]{1,0:T(8,128)(2,1)} collective-permute-done((bf16[512,1024]{1,0:T(8,128)(2,1)}, bf16[512,1024]{1,0:T(8,128)(2,1)}, u32[]{:S(2)}, u32[]{:S(2)}) %collective-permute-start) | collective-permute-done | bytes 1048608 | tf_op jit(solution)/shard_map/ppermute | solution.py:412
  30.8 1.9 slice.78
  32.7 2.1 collective-permute-start.4
  34.7 1.9 slice.79
  36.6 1.5 collective-permute-start.5
  39.6 1.0 broadcast_multiply_fusion.refs_2_
  40.6 12.9 %collective-permute-done.4.refs_7_ = bf16[256,1024]{1,0:T(8,128)(2,1)} collective-permute-done((bf16[256,1024]{1,0:T(8,128)(2,1)}, bf16[256,1024]{1,0:T(8,128)(2,1)}, u32[]{:S(2)}, u32[]{:S(2)}) %collective-permute-start.4) | collective-permute-done | bytes 524320 | tf_op jit(solution)/shard_map/ppermute | solution.py:412
  53.5 1.7 collective-permute-done.5.refs_8_
  57.8 1.2 gather_fusion
  59.0 1.9 fusion.2.refs_1_
  60.9 6.7 %lift.2 = (f32[8,512,512]{2,1,0:T(8,128)}, f32[8,256,256]{2,1,0:T(8,128)}) custom-call(s32[2]{0:T(128)} %bitcast.138, bf16[1024,512]{1,0:T(8,128)(2,1)} %bitcast.122, bf16[1024,256]{1,0:T(8,128)(2,1)} %broadcast_multiply_fusion.refs_2_, bf16[512,1024]{1,0:T(8,128)(2,1)} %mul.147.refs_3_, bf16[512,1024]{1,0:T(8,128)(2,1)} %collective-permute-done.8.refs_4_), custom_call_target="tpu_custom_call" | custom-call | flops 1073741824 | bytes 4194304 | tf_op jit(solution)/shard_map/lift/pallas_call | solution.py:101
  67.7 1.5 convert_element_type.76.refs_0_
  69.2 3.0 %collective-permute-start.11 = (bf16[4,256,512]{2,1,0:T(8,128)(2,1)}, bf16[4,256,512]{2,1,0:T(8,128)(2,1)S(1)}, u32[]{:S(2)}, u32[]{:S(2)}) collective-permute-start(bf16[4,256,512]{2,1,0:T(8,128)(2,1)} %collective-permute-done.10.refs_6_), channel_id=1, source_target_pairs={{0,1},{1,0},{2,3},{3,2},{4,5},{5,4},{6,7},{7,6},{8,9},{9,8},{10,11... | collective-permute-start | bytes 3145736 | tf_op jit(solution)/shard_map/ppermute | solution.py:444
  72.2 9.9 %collective-permute-start.13 = (bf16[4,256,512]{2,1,0:T(8,128)(2,1)}, bf16[4,256,512]{2,1,0:T(8,128)(2,1)}, u32[]{:S(2)}, u32[]{:S(2)}) collective-permute-start(bf16[4,256,512]{2,1,0:T(8,128)(2,1)} %collective-permute-done.12.refs_8_), channel_id=1, source_target_pairs={{0,1},{1,0},{2,3},{3,2},{4,5},{5,4},{6,7},{7,6},{8,9},{9,8},{10,11... | collective-permute-start | bytes 3145736 | tf_op jit(solution)/shard_map/ppermute | solution.py:444
  82.9 11.8 %lift.3 = (f32[8,512,512]{2,1,0:T(8,128)}, f32[8,256,256]{2,1,0:T(8,128)}) custom-call(s32[6]{0:T(128)} %slice.60.refs_0_, bf16[1024,512]{1,0:T(8,128)(2,1)} %bitcast.123, bf16[1024,256]{1,0:T(8,128)(2,1)} %broadcast_multiply_fusion.refs_2_, bf16[512,1024]{1,0:T(8,128)(2,1)} %collective-permute-done.refs_3_, ...), custom_call_target="tpu_custom_call", output_to_operand_aliasing={{0}: (11, {}), {1}: (12, {})} | custom-call | flops 3221225472 | bytes 12582912 | tf_op jit(solution)/shard_map/lift/pallas_call | solution.py:101
  94.7 1.8 multiply_convert_fusion
  96.5 1.0 slice_bitcast_fusion.1
  97.5 8.8 %forward.1.refs_0_ = f32[8,256,256]{2,1,0:T(8,128)} custom-call(f32[32,8,16,128]{3,2,1,0:T(8,128)} %convert_element_type.76.refs_0_, bf16[256,256]{1,0:T(8,128)(2,1)} %constant.156.clone.refs_1_, bf16[256,256]{1,0:T(8,128)(2,1)} %constant.157.clone.refs_2_, bf16[256,256]{1,0:T(8,128)(2,1)} %constant.158.clone.refs_3_.refs_8_, ...), custom_call_target="tpu_custom_call" | custom-call | flops 1610612736 | bytes 4194304 | tf_op jit(solution)/shard_map/forward/pallas_call | solution.py:321
  106.9 1.3 collective-permute-start.23
  108.6 4.2 %collective-permute-done.22 = f16[256,256]{1,0:T(8,128)(2,1)S(1)} collective-permute-done((f16[256,256]{1,0:T(8,128)(2,1)S(1)}, f16[256,256]{1,0:T(8,128)(2,1)S(1)}, u32[]{:S(2)}, u32[]{:S(2)}) %collective-permute-start.22) | collective-permute-done | bytes 131104 | tf_op jit(solution)/shard_map/ppermute | solution.py:412
  113.5 5.4 %collective-permute-done.13.refs_9_ = bf16[4,256,512]{2,1,0:T(8,128)(2,1)} collective-permute-done((bf16[4,256,512]{2,1,0:T(8,128)(2,1)}, bf16[4,256,512]{2,1,0:T(8,128)(2,1)}, u32[]{:S(2)}, u32[]{:S(2)}) %collective-permute-start.13) | collective-permute-done | bytes 1048608 | tf_op jit(solution)/shard_map/ppermute | solution.py:444
  119.8 10.3 %route.1 = (bf16[2,256,512]{2,1,0:T(8,128)(2,1)}, bf16[2,256,512]{2,1,0:T(8,128)(2,1)}, bf16[2,256,512]{2,1,0:T(8,128)(2,1)}, bf16[2,256,512]{2,1,0:T(8,128)(2,1...) custom-call(s32[8]{0:T(128)} %copy-done.16, ...), custom_call_target="tpu_custom_call" | custom-call | flops 4194304 | bytes 16777216 | tf_op jit(solution)/shard_map/route/pallas_call | solution.py:179
  132.0 4.2 %all-to-all-start.1 = ((f32[32,1,512]{2,1,0:T(1,128)}), f32[32,1,512]{2,1,0:T(1,128)S(1)}, u32[]{:S(2)}, u32[]{:S(2)}) async-start(f32[32,1,512]{2,1,0:T(1,128)} %reshape.307), calls=%async_computation.1 | async-start | bytes 131072 | tf_op jit(solution)/shard_map/all_to_all | solution.py:30
  136.2 7.5 %all-to-all-done.1 = f32[32,1,512]{2,1,0:T(1,128)S(1)} async-done(((f32[32,1,512]{2,1,0:T(1,128)}), f32[32,1,512]{2,1,0:T(1,128)S(1)}, u32[]{:S(2)}, u32[]{:S(2)}) %all-to-all-start.1) | async-done | bytes 65568 | tf_op jit(solution)/shard_map/all_to_all | solution.py:30
  146.3 17.1 %inverse.1 = bf16[32,9,16,128]{3,2,1,0:T(8,128)(2,1)} custom-call(f32[8,256,256]{2,1,0:T(8,128)} %forward.1.refs_0_, f32[8,256,256]{2,1,0:T(8,128)} %fusion.2.refs_1_, f32[8,16,256]{2,1,0:T(8,128)} %convolution_bitcast_fusion.refs_2_, f32[256,16]{1,0:T(8,128)} %bitcast.131, f32[2,8,256]{2,1,0:T(8,128)} %bitcast.135, f32[2,256,128]{2,1,0:T(8,128)} %constant.161.clone.refs_5_, ...), custom_call_target="tpu_custom_call" | custom-call | flops 1610612736 | bytes 5242880 | tf_op jit(solution)/shard_map/inverse/pallas_call | solution.py:386
  163.4 2.8 %all-to-all-start.2 = ((bf16[32,9,16,128]{3,2,1,0:T(8,128)(2,1)}), bf16[32,9,16,128]{3,2,1,0:T(8,128)(2,1)S(1)}, u32[]{:S(2)}, u32[]{:S(2)}) async-start(bf16[32,9,16,128]{3,2,1,0:T(8,128)(2,1)} %inverse.1), calls=%async_computation.2 | async-start | bytes 2359296 | tf_op jit(solution)/shard_map/all_to_all | solution.py:30
  170.6 1.6 collective-permute-start.28
  172.2 2.5 collective-permute-start.29
  175.1 17.2 %collective-permute-done.28 = f16[2,256,256]{2,1,0:T(8,128)(2,1)S(1)} collective-permute-done((f16[2,256,256]{2,1,0:T(8,128)(2,1)S(1)}, f16[2,256,256]{2,1,0:T(8,128)(2,1)S(1)}, u32[]{:S(2)}, u32[]{:S(2)}) %collective-permute-start.28) | collective-permute-done | bytes 262176 | tf_op jit(solution)/shard_map/ppermute | solution.py:663
  192.3 20.3 %collective-permute-done.29 = f16[2,256,256]{2,1,0:T(8,128)(2,1)S(1)} collective-permute-done((f16[2,256,256]{2,1,0:T(8,128)(2,1)S(1)}, f16[2,256,256]{2,1,0:T(8,128)(2,1)S(1)}, u32[]{:S(2)}, u32[]{:S(2)}) %collective-permute-start.29) | collective-permute-done | bytes 262176 | tf_op jit(solution)/shard_map/ppermute | solution.py:663
  213.4 1.5 collective-permute-start.15
  215.3 1.5 collective-permute-start.17
  218.6 2.4 collective-permute-start.19
  221.0 7.6 %collective-permute-done.15.refs_6_ = bf16[2,256,512]{2,1,0:T(8,128)(2,1)} collective-permute-done((bf16[2,256,512]{2,1,0:T(8,128)(2,1)}, bf16[2,256,512]{2,1,0:T(8,128)(2,1)}, u32[]{:S(2)}, u32[]{:S(2)}) %collective-permute-start.15) | collective-permute-done | bytes 524320 | tf_op jit(solution)/shard_map/ppermute | solution.py:412
  228.6 1.2 collective-permute-start.20
  231.0 2.0 fusion.24
  233.1 5.8 %collective-permute-done.16.refs_7_ = bf16[2,256,512]{2,1,0:T(8,128)(2,1)} collective-permute-done((bf16[2,256,512]{2,1,0:T(8,128)(2,1)}, bf16[2,256,512]{2,1,0:T(8,128)(2,1)}, u32[]{:S(2)}, u32[]{:S(2)}) %collective-permute-start.16) | collective-permute-done | bytes 524320 | tf_op jit(solution)/shard_map/ppermute | solution.py:412
  238.9 23.6 %collective-permute-done.18.refs_9_ = bf16[2,256,512]{2,1,0:T(8,128)(2,1)} collective-permute-done((bf16[2,256,512]{2,1,0:T(8,128)(2,1)}, bf16[2,256,512]{2,1,0:T(8,128)(2,1)}, u32[]{:S(2)}, u32[]{:S(2)}) %collective-permute-start.18) | collective-permute-done | bytes 524320 | tf_op jit(solution)/shard_map/ppermute | solution.py:412
  262.5 11.2 %hartree.1 = bf16[512,1024]{1,0:T(8,128)(2,1)} custom-call(s32[8]{0:T(128)} %copy-done.16, s32[2,4]{1,0:T(2,128)} %refs_1_.2, f32[2,4096]{1,0:T(2,128)} %bitcast.136, bf16[1024,4096]{1,0:T(8,128)(2,1)} %bitcast.134, bf16[2,256,512]{2,1,0:T(8,128)(2,1)} %get-tuple-element.20.refs_4_, bf16[2,256,512]{2,1,0:T(8,128)(2,1)} %collective-permute-done.14.refs_5_, ...), custom_call_target="tpu_custom_call" | custom-call | flops 4294967296 | bytes 12582912 | tf_op jit(solution)/shard_map/hartree/pallas_call | solution.py:236
  (144 shorter events, 24.3 us)
Async XLA Ops:
  0.6 10.3 %copy-start = (f32[32,64,256]{2,1,0:T(8,128)S(1)}, f32[32,64,256]{2,1,0:T(8,128)}, u32[]{:S(2)}) copy-start(f32[32,64,256]{2,1,0:T(8,128)} %param.26) | copy-start | bytes 6291460
  2.1 8.8 %copy-start.5 = (f32[256,256]{1,0:T(8,128)S(1)}, f32[256,256]{1,0:T(8,128)}, u32[]{:S(2)}) copy-start(f32[256,256]{1,0:T(8,128)} %constant.155.clone) | copy-start | bytes 786436
  3.5 35.3 %collective-permute-start.8 = (bf16[512,1024]{1,0:T(8,128)(2,1)}, bf16[512,1024]{1,0:T(8,128)(2,1)}, u32[]{:S(2)}, u32[]{:S(2)}) collective-permute-start(bf16[512,1024]{1,0:T(8,128)(2,1)} %mul.147.refs_3_), channel_id=1, source_target_pairs={{0,4},{1,5},{2,6},{3,7},{4,0},{5,1},{6,2},{7,3},{8,12},{9,13},{10,... | collective-permute-start | bytes 3145736 | tf_op jit(solution)/shard_map/ppermute | solution.py:412
  4.0 26.8 %collective-permute-start = (bf16[512,1024]{1,0:T(8,128)(2,1)}, bf16[512,1024]{1,0:T(8,128)(2,1)}, u32[]{:S(2)}, u32[]{:S(2)}) collective-permute-start(bf16[512,1024]{1,0:T(8,128)(2,1)} %mul.147.refs_3_), channel_id=1, source_target_pairs={{0,8},{1,9},{2,10},{3,11},{4,12},{5,13},{6,14},{7,15},{8,0},{9,1},... | collective-permute-start | bytes 3145736 | tf_op jit(solution)/shard_map/ppermute | solution.py:412
  6.4 28.3 %collective-permute-start.2 = (bf16[512,1024]{1,0:T(8,128)(2,1)}, bf16[512,1024]{1,0:T(8,128)(2,1)}, u32[]{:S(2)}, u32[]{:S(2)}) collective-permute-start(bf16[512,1024]{1,0:T(8,128)(2,1)} %mul.147.refs_3_), channel_id=1, source_target_pairs={{0,16},{1,17},{2,18},{3,19},{4,20},{5,21},{6,22},{7,23},{8,24},{9,... | collective-permute-start | bytes 3145736 | tf_op jit(solution)/shard_map/ppermute | solution.py:412
  9.3 29.6 %collective-permute-start.9 = (bf16[4,256,512]{2,1,0:T(8,128)(2,1)S(1)}, bf16[4,256,512]{2,1,0:T(8,128)(2,1)}, u32[]{:S(2)}, u32[]{:S(2)}) collective-permute-start(bf16[4,256,512]{2,1,0:T(8,128)(2,1)S(1)} %constant_dynamic-slice_fusion.refs_4_), channel_id=1, source_target_pairs={{0,1},{1,0},{2,3},{3,2},{4,5},{5,4},{6,7},{7,6},{8,9},{9,8},{10,11... | collective-permute-start | bytes 3145736 | tf_op jit(solution)/shard_map/ppermute | solution.py:444
  10.9 28.5 %collective-permute-start.10 = (bf16[4,256,512]{2,1,0:T(8,128)(2,1)S(1)}, bf16[4,256,512]{2,1,0:T(8,128)(2,1)}, u32[]{:S(2)}, u32[]{:S(2)}) collective-permute-start(bf16[4,256,512]{2,1,0:T(8,128)(2,1)S(1)} %constant_dynamic-slice_fusion.refs_4_), channel_id=1, source_target_pairs={{0,4},{1,2},{2,1},{3,7},{4,0},{5,6},{6,5},{7,3},{8,12},{9,10},{10,... | collective-permute-start | bytes 3145736 | tf_op jit(solution)/shard_map/ppermute | solution.py:444
  13.4 26.2 %copy-start.6 = (bf16[1024,256]{1,0:T(8,128)(2,1)S(1)}, bf16[1024,256]{1,0:T(8,128)(2,1)}, u32[]{:S(2)}) copy-start(bf16[1024,256]{1,0:T(8,128)(2,1)} %param.22) | copy-start | bytes 1572868
  13.4 54.3 %all-to-all-start = ((f16[32,8,16,128]{3,2,1,0:T(8,128)(2,1)}), f16[32,8,16,128]{3,2,1,0:T(8,128)(2,1)S(1)}, u32[]{:S(2)}, u32[]{:S(2)}) async-start(f16[32,8,16,128]{3,2,1,0:T(8,128)(2,1)} %bitcast.117), calls=%async_computation | async-start | bytes 2097152 | tf_op jit(solution)/shard_map/all_to_all | solution.py:30
  16.9 42.1 %copy-start.16 = (s32[8]{0:T(128)}, s32[8]{0:T(128)S(1)}, u32[]{:S(2)}) copy-start(s32[8]{0:T(128)S(1)} %iota_xor_fusion.refs_0_) | copy-start | bytes 100
  32.7 20.8 %collective-permute-start.4 = (bf16[256,1024]{1,0:T(8,128)(2,1)}, bf16[256,1024]{1,0:T(8,128)(2,1)}, u32[]{:S(2)}, u32[]{:S(2)}) collective-permute-start(bf16[256,1024]{1,0:T(8,128)(2,1)} %slice.78), channel_id=1, source_target_pairs={{0,16},{1,17},{2,18},{3,19},{4,20},{5,21},{6,22},{7,23},{8,24},{9,... | collective-permute-start | bytes 1572872 | tf_op jit(solution)/shard_map/ppermute | solution.py:412
  36.6 18.6 %collective-permute-start.5 = (bf16[256,1024]{1,0:T(8,128)(2,1)}, bf16[256,1024]{1,0:T(8,128)(2,1)}, u32[]{:S(2)}, u32[]{:S(2)}) collective-permute-start(bf16[256,1024]{1,0:T(8,128)(2,1)} %slice.79), channel_id=1, source_target_pairs={{0,8},{1,9},{2,10},{3,11},{4,12},{5,13},{6,14},{7,15},{8,0},{9,1},... | collective-permute-start | bytes 1572872 | tf_op jit(solution)/shard_map/ppermute | solution.py:412
  38.8 43.3 %collective-permute-start.1 = (bf16[512,1024]{1,0:T(8,128)(2,1)}, bf16[512,1024]{1,0:T(8,128)(2,1)}, u32[]{:S(2)}, u32[]{:S(2)}) collective-permute-start(bf16[512,1024]{1,0:T(8,128)(2,1)} %collective-permute-done.refs_3_), channel_id=1, source_target_pairs={{0,4},{1,5},{2,6},{3,7},{4,0},{5,1},{6,2},{7,3},{8,12},{9,13},{10,... | collective-permute-start | bytes 3145736 | tf_op jit(solution)/shard_map/ppermute | solution.py:412
  38.9 43.2 %collective-permute-start.3 = (bf16[512,1024]{1,0:T(8,128)(2,1)}, bf16[512,1024]{1,0:T(8,128)(2,1)}, u32[]{:S(2)}, u32[]{:S(2)}) collective-permute-start(bf16[512,1024]{1,0:T(8,128)(2,1)} %collective-permute-done.2.refs_5_), channel_id=1, source_target_pairs={{0,4},{1,5},{2,6},{3,7},{4,0},{5,1},{6,2},{7,3},{8,12},{9,13},{10,... | collective-permute-start | bytes 3145736 | tf_op jit(solution)/shard_map/ppermute | solution.py:412
  39.4 32.8 %collective-permute-start.12 = (bf16[4,256,512]{2,1,0:T(8,128)(2,1)}, bf16[4,256,512]{2,1,0:T(8,128)(2,1)}, u32[]{:S(2)}, u32[]{:S(2)}) collective-permute-start(bf16[4,256,512]{2,1,0:T(8,128)(2,1)} %collective-permute-done.9.refs_5_), channel_id=1, source_target_pairs={{0,4},{1,2},{2,1},{3,7},{4,0},{5,6},{6,5},{7,3},{8,12},{9,10},{10,... | collective-permute-start | bytes 3145736 | tf_op jit(solution)/shard_map/ppermute | solution.py:444
  53.5 15.8 %collective-permute-start.6 = (bf16[256,1024]{1,0:T(8,128)(2,1)}, bf16[256,1024]{1,0:T(8,128)(2,1)S(1)}, u32[]{:S(2)}, u32[]{:S(2)}) collective-permute-start(bf16[256,1024]{1,0:T(8,128)(2,1)} %collective-permute-done.4.refs_7_), channel_id=1, source_target_pairs={{0,4},{1,5},{2,6},{3,7},{4,0},{5,1},{6,2},{7,3},{8,12},{9,13},{10,... | collective-permute-start | bytes 1572872 | tf_op jit(solution)/shard_map/ppermute | solution.py:412
  55.1 27.0 %collective-permute-start.7 = (bf16[256,1024]{1,0:T(8,128)(2,1)}, bf16[256,1024]{1,0:T(8,128)(2,1)S(1)}, u32[]{:S(2)}, u32[]{:S(2)}) collective-permute-start(bf16[256,1024]{1,0:T(8,128)(2,1)} %collective-permute-done.5.refs_8_), channel_id=1, source_target_pairs={{0,4},{1,5},{2,6},{3,7},{4,0},{5,1},{6,2},{7,3},{8,12},{9,13},{10,... | collective-permute-start | bytes 1572872 | tf_op jit(solution)/shard_map/ppermute | solution.py:412
  69.2 12.9 %copy-start.7 = (bf16[256,1024]{1,0:T(8,128)(2,1)}, bf16[256,1024]{1,0:T(8,128)(2,1)S(1)}, u32[]{:S(2)}) copy-start(bf16[256,1024]{1,0:T(8,128)(2,1)S(1)} %collective-permute-done.6.refs_9_) | copy-start | bytes 1572868
  69.2 43.5 %collective-permute-start.11 = (bf16[4,256,512]{2,1,0:T(8,128)(2,1)}, bf16[4,256,512]{2,1,0:T(8,128)(2,1)S(1)}, u32[]{:S(2)}, u32[]{:S(2)}) collective-permute-start(bf16[4,256,512]{2,1,0:T(8,128)(2,1)} %collective-permute-done.10.refs_6_), channel_id=1, source_target_pairs={{0,1},{1,0},{2,3},{3,2},{4,5},{5,4},{6,7},{7,6},{8,9},{9,8},{10,11... | collective-permute-start | bytes 3145736 | tf_op jit(solution)/shard_map/ppermute | solution.py:444
  72.2 46.6 %collective-permute-start.13 = (bf16[4,256,512]{2,1,0:T(8,128)(2,1)}, bf16[4,256,512]{2,1,0:T(8,128)(2,1)}, u32[]{:S(2)}, u32[]{:S(2)}) collective-permute-start(bf16[4,256,512]{2,1,0:T(8,128)(2,1)} %collective-permute-done.12.refs_8_), channel_id=1, source_target_pairs={{0,1},{1,0},{2,3},{3,2},{4,5},{5,4},{6,7},{7,6},{8,9},{9,8},{10,11... | collective-permute-start | bytes 3145736 | tf_op jit(solution)/shard_map/ppermute | solution.py:444
  97.5 8.8 %copy-start.11 = (f16[256,256]{1,0:T(8,128)(2,1)S(1)}, f16[256,256]{1,0:T(8,128)(2,1)}, u32[]{:S(2)}) copy-start(f16[256,256]{1,0:T(8,128)(2,1)} %get-tuple-element.37) | copy-start | bytes 393220
  97.5 9.3 %copy-start.10 = (f16[256,256]{1,0:T(8,128)(2,1)S(1)}, f16[256,256]{1,0:T(8,128)(2,1)}, u32[]{:S(2)}) copy-start(f16[256,256]{1,0:T(8,128)(2,1)} %get-tuple-element.36) | copy-start | bytes 393220
  97.5 10.6 %collective-permute-start.21 = (f16[256,256]{1,0:T(8,128)(2,1)}, f16[256,256]{1,0:T(8,128)(2,1)S(1)}, u32[]{:S(2)}, u32[]{:S(2)}) collective-permute-start(f16[256,256]{1,0:T(8,128)(2,1)} %get-tuple-element.38), channel_id=1, source_target_pairs={{0,4},{1,5},{2,6},{3,7},{4,0},{5,1},{6,2},{7,3},{8,12},{9,13},{10,... | collective-permute-start | bytes 393224 | tf_op jit(solution)/shard_map/ppermute | solution.py:412
  106.4 6.4 %collective-permute-start.22 = (f16[256,256]{1,0:T(8,128)(2,1)S(1)}, f16[256,256]{1,0:T(8,128)(2,1)S(1)}, u32[]{:S(2)}, u32[]{:S(2)}) collective-permute-start(f16[256,256]{1,0:T(8,128)(2,1)S(1)} %copy-done.11), channel_id=1, source_target_pairs={{0,8},{1,9},{2,10},{3,11},{4,12},{5,13},{6,14},{7,15},{8,0},{9,1},... | collective-permute-start | bytes 393224 | tf_op jit(solution)/shard_map/ppermute | solution.py:412
  106.9 29.3 %collective-permute-start.23 = (f16[256,256]{1,0:T(8,128)(2,1)S(1)}, f16[256,256]{1,0:T(8,128)(2,1)S(1)}, u32[]{:S(2)}, u32[]{:S(2)}) collective-permute-start(f16[256,256]{1,0:T(8,128)(2,1)S(1)} %copy-done.10), channel_id=1, source_target_pairs={{0,12},{1,13},{2,14},{3,15},{4,8},{5,9},{6,10},{7,11},{8,4},{9,5},... | collective-permute-start | bytes 393224 | tf_op jit(solution)/shard_map/ppermute | solution.py:412
  108.1 58.2 %collective-permute-start.24 = (f16[256,256]{1,0:T(8,128)(2,1)}, f16[256,256]{1,0:T(8,128)(2,1)}, u32[]{:S(2)}, u32[]{:S(2)}) collective-permute-start(f16[256,256]{1,0:T(8,128)(2,1)} %get-tuple-element.35), channel_id=1, source_target_pairs={{0,16},{1,17},{2,18},{3,19},{4,20},{5,21},{6,22},{7,23},{8,24},{9,... | collective-permute-start | bytes 393224 | tf_op jit(solution)/shard_map/ppermute | solution.py:412
  112.7 54.5 %collective-permute-start.25 = (f16[256,256]{1,0:T(8,128)(2,1)S(1)}, f16[256,256]{1,0:T(8,128)(2,1)}, u32[]{:S(2)}, u32[]{:S(2)}) collective-permute-start(f16[256,256]{1,0:T(8,128)(2,1)S(1)} %get-tuple-element.34), channel_id=1, source_target_pairs={{0,20},{1,21},{2,22},{3,23},{4,16},{5,17},{6,18},{7,19},{8,28},{9,... | collective-permute-start | bytes 393224 | tf_op jit(solution)/shard_map/ppermute | solution.py:412
  112.8 7.0 %copy-start.4 = (bf16[4,256,512]{2,1,0:T(8,128)(2,1)}, bf16[4,256,512]{2,1,0:T(8,128)(2,1)S(1)}, u32[]{:S(2)}) copy-start(bf16[4,256,512]{2,1,0:T(8,128)(2,1)S(1)} %collective-permute-done.11.refs_7_) | copy-start | bytes 3145732
  112.8 55.4 %collective-permute-start.26 = (f16[256,256]{1,0:T(8,128)(2,1)S(1)}, f16[256,256]{1,0:T(8,128)(2,1)}, u32[]{:S(2)}, u32[]{:S(2)}) collective-permute-start(f16[256,256]{1,0:T(8,128)(2,1)S(1)} %get-tuple-element.33), channel_id=1, source_target_pairs={{0,24},{1,25},{2,26},{3,27},{4,28},{5,29},{6,30},{7,31},{8,16},{9,... | collective-permute-start | bytes 393224 | tf_op jit(solution)/shard_map/ppermute | solution.py:412
  118.9 50.3 %collective-permute-start.27 = (f16[256,256]{1,0:T(8,128)(2,1)S(1)}, f16[256,256]{1,0:T(8,128)(2,1)}, u32[]{:S(2)}, u32[]{:S(2)}) collective-permute-start(f16[256,256]{1,0:T(8,128)(2,1)S(1)} %get-tuple-element.32), channel_id=1, source_target_pairs={{0,28},{1,29},{2,30},{3,31},{4,24},{5,25},{6,26},{7,27},{8,20},{9,... | collective-permute-start | bytes 393224 | tf_op jit(solution)/shard_map/ppermute | solution.py:412
  119.8 11.2 %copy-start.13 = (f32[128,256]{1,0:T(8,128)S(1)}, f32[128,256]{1,0:T(8,128)}, u32[]{:S(2)}) copy-start(f32[128,256]{1,0:T(8,128)} %constant.153.clone) | copy-start | bytes 393220
  130.1 15.2 %copy-start.14 = (f32[32,256,1]{1,0,2:T(8,128)S(1)}, f32[32,256,1]{1,0,2:T(8,128)}, u32[]{:S(2)}) copy-start(f32[32,256,1]{1,0,2:T(8,128)} %constant.168) | copy-start | bytes 98308
  132.0 11.7 %all-to-all-start.1 = ((f32[32,1,512]{2,1,0:T(1,128)}), f32[32,1,512]{2,1,0:T(1,128)S(1)}, u32[]{:S(2)}, u32[]{:S(2)}) async-start(f32[32,1,512]{2,1,0:T(1,128)} %reshape.307), calls=%async_computation.1 | async-start | bytes 131072 | tf_op jit(solution)/shard_map/all_to_all | solution.py:30
  163.4 53.5 %all-to-all-start.2 = ((bf16[32,9,16,128]{3,2,1,0:T(8,128)(2,1)}), bf16[32,9,16,128]{3,2,1,0:T(8,128)(2,1)S(1)}, u32[]{:S(2)}, u32[]{:S(2)}) async-start(bf16[32,9,16,128]{3,2,1,0:T(8,128)(2,1)} %inverse.1), calls=%async_computation.2 | async-start | bytes 2359296 | tf_op jit(solution)/shard_map/all_to_all | solution.py:30
  170.6 47.0 %copy-start.12 = (f32[128,256,1]{1,0,2:T(8,128)S(1)}, f32[128,256,1]{1,0,2:T(8,128)}, u32[]{:S(2)}) copy-start(f32[128,256,1]{1,0,2:T(8,128)} %constant.170) | copy-start | bytes 393220
  170.6 48.0 %copy-start.18 = (bf16[2,256,512]{2,1,0:T(8,128)(2,1)S(1)}, bf16[2,256,512]{2,1,0:T(8,128)(2,1)}, u32[]{:S(2)}) copy-start(bf16[2,256,512]{2,1,0:T(8,128)(2,1)} %get-tuple-element.26) | copy-start | bytes 1572868
  170.6 58.0 %copy-start.17 = (bf16[2,256,512]{2,1,0:T(8,128)(2,1)S(1)}, bf16[2,256,512]{2,1,0:T(8,128)(2,1)}, u32[]{:S(2)}) copy-start(bf16[2,256,512]{2,1,0:T(8,128)(2,1)} %get-tuple-element.27) | copy-start | bytes 1572868
  170.6 21.6 %collective-permute-start.28 = (f16[2,256,256]{2,1,0:T(8,128)(2,1)S(1)}, f16[2,256,256]{2,1,0:T(8,128)(2,1)S(1)}, u32[]{:S(2)}, u32[]{:S(2)}) collective-permute-start(f16[2,256,256]{2,1,0:T(8,128)(2,1)S(1)} %get-tuple-element.29), channel_id=1, source_target_pairs={{0,1},{1,0},{2,3},{3,2},{4,5},{5,4},{6,7},{7,6},{8,9},{9,8},{10,11... | collective-permute-start | bytes 786440 | tf_op jit(solution)/shard_map/ppermute | solution.py:663
  172.2 40.3 %collective-permute-start.29 = (f16[2,256,256]{2,1,0:T(8,128)(2,1)S(1)}, f16[2,256,256]{2,1,0:T(8,128)(2,1)S(1)}, u32[]{:S(2)}, u32[]{:S(2)}) collective-permute-start(f16[2,256,256]{2,1,0:T(8,128)(2,1)S(1)} %get-tuple-element.31), channel_id=1, source_target_pairs={{0,2},{1,3},{2,0},{3,1},{4,6},{5,7},{6,4},{7,5},{8,10},{9,11},{10,... | collective-permute-start | bytes 786440 | tf_op jit(solution)/shard_map/ppermute | solution.py:663
  174.7 37.8 %collective-permute-start.30 = (f16[2,256,256]{2,1,0:T(8,128)(2,1)S(1)}, f16[2,256,256]{2,1,0:T(8,128)(2,1)S(1)}, u32[]{:S(2)}, u32[]{:S(2)}) collective-permute-start(f16[2,256,256]{2,1,0:T(8,128)(2,1)S(1)} %get-tuple-element.30), channel_id=1, source_target_pairs={{0,3},{1,2},{2,1},{3,0},{4,7},{5,6},{6,5},{7,4},{8,11},{9,10},{10,... | collective-permute-start | bytes 786440 | tf_op jit(solution)/shard_map/ppermute | solution.py:663
  213.4 5.1 %collective-permute-start.14 = (bf16[2,256,512]{2,1,0:T(8,128)(2,1)}, bf16[2,256,512]{2,1,0:T(8,128)(2,1)}, u32[]{:S(2)}, u32[]{:S(2)}) collective-permute-start(bf16[2,256,512]{2,1,0:T(8,128)(2,1)} %get-tuple-element.21), channel_id=1, source_target_pairs={{0,4},{1,5},{2,6},{3,7},{4,0},{5,1},{6,2},{7,3},{8,12},{9,13},{10,... | collective-permute-start | bytes 1572872 | tf_op jit(solution)/shard_map/ppermute | solution.py:412
  213.4 15.1 %collective-permute-start.15 = (bf16[2,256,512]{2,1,0:T(8,128)(2,1)}, bf16[2,256,512]{2,1,0:T(8,128)(2,1)}, u32[]{:S(2)}, u32[]{:S(2)}) collective-permute-start(bf16[2,256,512]{2,1,0:T(8,128)(2,1)} %get-tuple-element.22), channel_id=1, source_target_pairs={{0,8},{1,9},{2,10},{3,11},{4,12},{5,13},{6,14},{7,15},{8,0},{9,1},... | collective-permute-start | bytes 1572872 | tf_op jit(solution)/shard_map/ppermute | solution.py:412
  214.9 23.9 %collective-permute-start.16 = (bf16[2,256,512]{2,1,0:T(8,128)(2,1)}, bf16[2,256,512]{2,1,0:T(8,128)(2,1)}, u32[]{:S(2)}, u32[]{:S(2)}) collective-permute-start(bf16[2,256,512]{2,1,0:T(8,128)(2,1)} %get-tuple-element.23), channel_id=1, source_target_pairs={{0,12},{1,13},{2,14},{3,15},{4,8},{5,9},{6,10},{7,11},{8,4},{9,5},... | collective-permute-start | bytes 1572872 | tf_op jit(solution)/shard_map/ppermute | solution.py:412
  215.3 23.6 %collective-permute-start.17 = (bf16[2,256,512]{2,1,0:T(8,128)(2,1)}, bf16[2,256,512]{2,1,0:T(8,128)(2,1)}, u32[]{:S(2)}, u32[]{:S(2)}) collective-permute-start(bf16[2,256,512]{2,1,0:T(8,128)(2,1)} %get-tuple-element.24), channel_id=1, source_target_pairs={{0,16},{1,17},{2,18},{3,19},{4,20},{5,21},{6,22},{7,23},{8,24},{9,... | collective-permute-start | bytes 1572872 | tf_op jit(solution)/shard_map/ppermute | solution.py:412
  216.8 45.7 %collective-permute-start.18 = (bf16[2,256,512]{2,1,0:T(8,128)(2,1)}, bf16[2,256,512]{2,1,0:T(8,128)(2,1)}, u32[]{:S(2)}, u32[]{:S(2)}) collective-permute-start(bf16[2,256,512]{2,1,0:T(8,128)(2,1)} %get-tuple-element.25), channel_id=1, source_target_pairs={{0,20},{1,21},{2,22},{3,23},{4,16},{5,17},{6,18},{7,19},{8,28},{9,... | collective-permute-start | bytes 1572872 | tf_op jit(solution)/shard_map/ppermute | solution.py:412
  218.6 43.9 %collective-permute-start.19 = (bf16[2,256,512]{2,1,0:T(8,128)(2,1)S(1)}, bf16[2,256,512]{2,1,0:T(8,128)(2,1)}, u32[]{:S(2)}, u32[]{:S(2)}) collective-permute-start(bf16[2,256,512]{2,1,0:T(8,128)(2,1)S(1)} %copy-done.18), channel_id=1, source_target_pairs={{0,24},{1,25},{2,26},{3,27},{4,28},{5,29},{6,30},{7,31},{8,16},{9,... | collective-permute-start | bytes 1572872 | tf_op jit(solution)/shard_map/ppermute | solution.py:412
  228.6 33.9 %collective-permute-start.20 = (bf16[2,256,512]{2,1,0:T(8,128)(2,1)S(1)}, bf16[2,256,512]{2,1,0:T(8,128)(2,1)}, u32[]{:S(2)}, u32[]{:S(2)}) collective-permute-start(bf16[2,256,512]{2,1,0:T(8,128)(2,1)S(1)} %copy-done.17), channel_id=1, source_target_pairs={{0,28},{1,29},{2,30},{3,31},{4,24},{5,25},{6,26},{7,27},{8,20},{9,... | collective-permute-start | bytes 1572872 | tf_op jit(solution)/shard_map/ppermute | solution.py:412
  262.5 11.3 %copy-start.1 = (f32[32,64,256]{2,1,0:T(8,128)S(1)}, f32[32,64,256]{2,1,0:T(8,128)}, u32[]{:S(2)}) copy-start(f32[32,64,256]{2,1,0:T(8,128)} %param.26) | copy-start | bytes 6291460
  (8 other events, 29.8 us)
